TPU v7x, 128 devices: a whole 4x4x4 slice. The times are simulated.
128 devices in a mesh: query: 8 (over x, z_hi), tok: 16 (over y, z_lo, core).
Axes of the slice: x: 4, y: 4, z: 4 (z_hi: 2, z_lo: 2; z = z_hi * 2 + z_lo), core: 2. Of those that a mesh axis runs over, the one named last changes fastest.
Arguments:
- queries: bfloat16 [32768, 128], P('query'), may hold values from -16 to 16, as said below
- documents: bfloat16 [32768, 128], P('tok'), may hold values from -10 to 10, as said below
- cotangent: float32 [1024], P('query'), may hold values from -6 to 6
Outputs:
- grad_queries: float32 [32768, 128], P(('query', 'tok'))
- grad_documents: float32 [16, 2048, 128], P('tok', 'query')
Inputs may be any that keep to these rules, and one draw needn't show every extreme that they name: `documents`: document embeddings of order one. `queries`: query embeddings of order one.
All inputs are finite; a program needn't handle non-finite values.
Results may differ from a plain program's by a relative error of at most 0.0029.
Values may be sent and summed in bfloat16 or wider, within the bound.
A program may use at most 64 MiB of HBM per device.

v0:
```python
import jax
import jax.numpy as jnp
from jax import lax
from jax.sharding import PartitionSpec as P

QLEN = 32


inv_temp = 2.0


def score_rows(q_rows, doc_rows):
    return (
        lax.dot_general(
            q_rows, doc_rows, (((1,), (1,)), ((), ())), preferred_element_type=jnp.float32
        )
        * inv_temp
    )


def shards(queries, documents, cotangent):
    n_rows, feat_width = queries.shape
    n_docs = documents.shape[0]
    blk_rows = min(512, n_rows)
    n_blocks = n_rows // blk_rows
    row_weight = jnp.broadcast_to(cotangent[:, None], (cotangent.shape[0], QLEN)).reshape(-1)
    q_blocks = queries.reshape(n_blocks, blk_rows, feat_width)

    def local_stats(carry, q_rows):
        scores = score_rows(q_rows, documents)
        row_top = jnp.max(scores, axis=1)
        row_total = jnp.sum(jnp.exp(scores - row_top[:, None]), axis=1)
        return (carry, (row_top, row_total))

    _, (row_tops, row_totals) = lax.scan(local_stats, 0, q_blocks)
    row_tops = row_tops.reshape(-1)
    row_totals = row_totals.reshape(-1)
    top_all = lax.pmax(row_tops, "tok")
    total_all = lax.psum(row_totals * jnp.exp(row_tops - top_all), "tok")
    log_total = top_all + jnp.log(total_all)
    log_blocks = log_total.reshape(n_blocks, blk_rows)
    weight_blocks = row_weight.reshape(n_blocks, blk_rows)

    def backward_both(doc_total, inputs_blk):
        q_rows, log_rows, weight_rows = inputs_blk
        scores = score_rows(q_rows, documents)
        probs = jnp.exp(scores - log_rows[:, None])
        weights_low = probs.astype(jnp.bfloat16)
        grad_rows = weight_rows[:, None] * jnp.dot(
            weights_low, documents, preferred_element_type=jnp.float32
        )
        scaled = (weight_rows[:, None] * probs).astype(jnp.bfloat16)
        doc_total = doc_total + lax.dot_general(
            scaled, q_rows, (((0,), (0,)), ((), ())), preferred_element_type=jnp.float32
        )
        return (doc_total, grad_rows)

    doc_total, grad_blocks = lax.scan(
        backward_both,
        jnp.zeros((n_docs, feat_width), jnp.float32),
        (q_blocks, log_blocks, weight_blocks),
    )
    grad_docs = lax.psum_scatter(doc_total, "query", scatter_dimension=0, tiled=True)
    query_terms = grad_blocks.reshape(n_rows, feat_width)
    grad_q = lax.psum_scatter(query_terms, "tok", scatter_dimension=0, tiled=True)
    return (grad_q, grad_docs[None])


def solution(mesh):
    placed = (P("query", None), P("tok", None), P("query"))
    return jax.shard_map(
        shards,
        mesh=mesh,
        in_specs=placed,
        out_specs=(P(("query", "tok"), None), P("tok", "query", None)),
        check_vma=False,
    )
```

profile of v0, /device:TPU:1, one launch (start us, length us, event | category | flops | bytes accessed | tf_op | source)
XLA Modules:
  0.0 356.0 jit_solution(10717387732099525368)
XLA Ops:
  7.3 23.1 %while.25 = (s32[]{:T(128)}, f32[8,512]{1,0:T(8,128)S(1)}, f32[8,512]{1,0:T(8,128)S(1)}, bf16[8,512,128]{2,1,0:T(8,128)(2,1)}, bf16[2048,128]{1,0:T(8,128)(2,1)}, /*index=5*/s32[]{:T(128)}, s32[]{:T(128)}) while((s32[]{:T(128)}, f32[8,512]{1,0:T(8,128)S(1)}, f32[8,512]{1,0:T(8,128)S(1)}, bf16[8,512,128]{2,1,0:T(8,128)(2,1)}, ...), condition=%wide.region_3.4_spmd, body=%wide.region_0.3_spmd.sunk | while | flops 273677312 | bytes 9058901 | solution.py:35
  7.3 1.9 multiply_reduce_fusion.2
  9.2 0.8 exponential_reduce_fusion.2
  10.2 1.9 multiply_reduce_fusion.2
  13.0 1.9 multiply_reduce_fusion.2
  15.9 1.9 multiply_reduce_fusion.2
  18.8 1.9 multiply_reduce_fusion.2
  21.7 1.9 multiply_reduce_fusion.2
  24.6 1.9 multiply_reduce_fusion.2
  27.5 1.9 multiply_reduce_fusion.2
  30.3 53.6 %pmax.7 = f32[4096]{0:T(1024)S(1)} all-reduce(f32[4096]{0:T(1024)S(1)} %bitcast.57), channel_id=1, replica_groups=mesh['query'=8,'tok'=16] {'tok'}, use_global_device_ids=true, to_apply=%region_4.5 | all-reduce | flops 4096 | bytes 32768 | tf_op jit(solution)/shard_map/pmax | solution.py:38
  84.0 52.9 %psum.7 = f32[4096]{0:T(1024)S(1)} all-reduce(f32[4096]{0:T(1024)S(1)} %exponential_multiply_fusion), channel_id=1, replica_groups=mesh['query'=8,'tok'=16] {'tok'}, use_global_device_ids=true, to_apply=%region_5.6 | all-reduce | flops 4096 | bytes 32768 | tf_op jit(solution)/shard_map/psum | solution.py:39
  137.1 72.0 %while.26 = (s32[]{:T(128)}, f32[2048,128]{1,0:T(8,128)S(1)}, f32[8,512,128]{2,1,0:T(8,128)}, f32[8,512]{1,0:T(8,128)S(1)}, bf16[8,512,128]{2,1,0:T(8,128)(2,1)}...) while((s32[]{:T(128)}, f32[2048,128]{1,0:T(8,128)S(1)}, ...), condition=%wide.region_7.8_spmd.clone, body=%wide.region_6.7_spmd.clone.sunk | while | flops 813236224 | bytes 35145376 | solution.py:58
  137.2 1.9 fusion.46
  139.1 1.9 copy-done
  141.0 1.5 fusion.47
  142.5 3.6 %convolution_add_fusion.2 = f32[2048,128]{1,0:T(8,128)S(1)} fusion(f32[512,2048]{1,0:T(8,128)} %copy-done, f32[512]{0:T(512)S(1)} %bitcast.53, f32[512]{0:T(512)S(1)} %bitcast.55, f32[2048,128]{1,0:T(8,128)S(1)} %get-tuple-element.237, pred[]{:T(512)S(6)} %compare.3, bf16[8,512,128]{2,1,0:T(8,128)(2,1)} %get-tuple-element.249, s32[]{:T(128)} %get-tuple-element.236), kind=kOutput, calls=%fused_computation.9.clone.1 | convolution fusion | flops 273154048 | bytes 6427137 | tf_op jit(solution)/shard_map/while/body/eval_jaxpr/dot_general | solution.py:53
  146.2 1.9 fusion.46
  148.1 1.9 copy-done
  150.0 1.5 fusion.47
  151.5 3.6 %convolution_add_fusion.2 = f32[2048,128]{1,0:T(8,128)S(1)} fusion(f32[512,2048]{1,0:T(8,128)} %copy-done, f32[512]{0:T(512)S(1)} %bitcast.53, f32[512]{0:T(512)S(1)} %bitcast.55, f32[2048,128]{1,0:T(8,128)S(1)} %get-tuple-element.237, pred[]{:T(512)S(6)} %compare.3, bf16[8,512,128]{2,1,0:T(8,128)(2,1)} %get-tuple-element.249, s32[]{:T(128)} %get-tuple-element.236), kind=kOutput, calls=%fused_computation.9.clone.1 | convolution fusion | flops 273154048 | bytes 6427137 | tf_op jit(solution)/shard_map/while/body/eval_jaxpr/dot_general | solution.py:53
  155.1 1.9 fusion.46
  157.1 1.9 copy-done
  159.0 1.6 fusion.47
  160.5 3.6 %convolution_add_fusion.2 = f32[2048,128]{1,0:T(8,128)S(1)} fusion(f32[512,2048]{1,0:T(8,128)} %copy-done, f32[512]{0:T(512)S(1)} %bitcast.53, f32[512]{0:T(512)S(1)} %bitcast.55, f32[2048,128]{1,0:T(8,128)S(1)} %get-tuple-element.237, pred[]{:T(512)S(6)} %compare.3, bf16[8,512,128]{2,1,0:T(8,128)(2,1)} %get-tuple-element.249, s32[]{:T(128)} %get-tuple-element.236), kind=kOutput, calls=%fused_computation.9.clone.1 | convolution fusion | flops 273154048 | bytes 6427137 | tf_op jit(solution)/shard_map/while/body/eval_jaxpr/dot_general | solution.py:53
  164.1 1.9 fusion.46
  166.1 1.9 copy-done
  168.0 1.6 fusion.47
  169.5 3.6 %convolution_add_fusion.2 = f32[2048,128]{1,0:T(8,128)S(1)} fusion(f32[512,2048]{1,0:T(8,128)} %copy-done, f32[512]{0:T(512)S(1)} %bitcast.53, f32[512]{0:T(512)S(1)} %bitcast.55, f32[2048,128]{1,0:T(8,128)S(1)} %get-tuple-element.237, pred[]{:T(512)S(6)} %compare.3, bf16[8,512,128]{2,1,0:T(8,128)(2,1)} %get-tuple-element.249, s32[]{:T(128)} %get-tuple-element.236), kind=kOutput, calls=%fused_computation.9.clone.1 | convolution fusion | flops 273154048 | bytes 6427137 | tf_op jit(solution)/shard_map/while/body/eval_jaxpr/dot_general | solution.py:53
  173.2 1.9 fusion.46
  175.1 1.9 copy-done
  177.0 1.5 fusion.47
  178.5 3.6 %convolution_add_fusion.2 = f32[2048,128]{1,0:T(8,128)S(1)} fusion(f32[512,2048]{1,0:T(8,128)} %copy-done, f32[512]{0:T(512)S(1)} %bitcast.53, f32[512]{0:T(512)S(1)} %bitcast.55, f32[2048,128]{1,0:T(8,128)S(1)} %get-tuple-element.237, pred[]{:T(512)S(6)} %compare.3, bf16[8,512,128]{2,1,0:T(8,128)(2,1)} %get-tuple-element.249, s32[]{:T(128)} %get-tuple-element.236), kind=kOutput, calls=%fused_computation.9.clone.1 | convolution fusion | flops 273154048 | bytes 6427137 | tf_op jit(solution)/shard_map/while/body/eval_jaxpr/dot_general | solution.py:53
  182.2 1.9 fusion.46
  184.1 1.9 copy-done
  186.0 1.6 fusion.47
  187.5 3.6 %convolution_add_fusion.2 = f32[2048,128]{1,0:T(8,128)S(1)} fusion(f32[512,2048]{1,0:T(8,128)} %copy-done, f32[512]{0:T(512)S(1)} %bitcast.53, f32[512]{0:T(512)S(1)} %bitcast.55, f32[2048,128]{1,0:T(8,128)S(1)} %get-tuple-element.237, pred[]{:T(512)S(6)} %compare.3, bf16[8,512,128]{2,1,0:T(8,128)(2,1)} %get-tuple-element.249, s32[]{:T(128)} %get-tuple-element.236), kind=kOutput, calls=%fused_computation.9.clone.1 | convolution fusion | flops 273154048 | bytes 6427137 | tf_op jit(solution)/shard_map/while/body/eval_jaxpr/dot_general | solution.py:53
  191.2 1.9 fusion.46
  193.1 1.9 copy-done
  195.0 1.6 fusion.47
  196.5 3.6 %convolution_add_fusion.2 = f32[2048,128]{1,0:T(8,128)S(1)} fusion(f32[512,2048]{1,0:T(8,128)} %copy-done, f32[512]{0:T(512)S(1)} %bitcast.53, f32[512]{0:T(512)S(1)} %bitcast.55, f32[2048,128]{1,0:T(8,128)S(1)} %get-tuple-element.237, pred[]{:T(512)S(6)} %compare.3, bf16[8,512,128]{2,1,0:T(8,128)(2,1)} %get-tuple-element.249, s32[]{:T(128)} %get-tuple-element.236), kind=kOutput, calls=%fused_computation.9.clone.1 | convolution fusion | flops 273154048 | bytes 6427137 | tf_op jit(solution)/shard_map/while/body/eval_jaxpr/dot_general | solution.py:53
  200.2 1.9 fusion.46
  202.1 1.9 copy-done
  204.0 1.6 fusion.47
  205.5 3.6 %convolution_add_fusion.2 = f32[2048,128]{1,0:T(8,128)S(1)} fusion(f32[512,2048]{1,0:T(8,128)} %copy-done, f32[512]{0:T(512)S(1)} %bitcast.53, f32[512]{0:T(512)S(1)} %bitcast.55, f32[2048,128]{1,0:T(8,128)S(1)} %get-tuple-element.237, pred[]{:T(512)S(6)} %compare.3, bf16[8,512,128]{2,1,0:T(8,128)(2,1)} %get-tuple-element.249, s32[]{:T(128)} %get-tuple-element.236), kind=kOutput, calls=%fused_computation.9.clone.1 | convolution fusion | flops 273154048 | bytes 6427137 | tf_op jit(solution)/shard_map/while/body/eval_jaxpr/dot_general | solution.py:53
  209.2 1.0 copy-done.2
  210.9 73.3 %reduce-scatter.5.cloned.1.call-done = f32[256,128]{1,0:T(8,128)} async-done(((f32[2048,128]{1,0:T(8,128)}), f32[256,128]{1,0:T(8,128)}) %reduce-scatter.5.cloned.1.call-update) | async-done | bytes 131088 | tf_op jit(solution)/shard_map/reduce_scatter | solution.py:63
  284.2 65.0 %reduce-scatter.3.cloned.1.call-done = f32[256,128]{1,0:T(8,128)} async-done(((f32[4096,128]{1,0:T(8,128)}), f32[256,128]{1,0:T(8,128)}) %reduce-scatter.3.cloned.1.call-update) | async-done | bytes 131088 | tf_op jit(solution)/shard_map/reduce_scatter | solution.py:65
  (74 shorter events, 8.0 us)
Async XLA Ops:
  7.2 277.0 %reduce-scatter.5.cloned.1.call-start = ((), (), s32[]{:S(2)}) async-start(), calls=%async_computation.3 | async-start | bytes 1179648 | tf_op jit(solution)/shard_map/reduce_scatter | solution.py:63
  7.2 129.6 %copy-start.3 = (f32[128]{0:T(128)S(1)}, f32[128]{0:T(128)}, u32[]{:S(2)}) copy-start(f32[128]{0:T(128)} %param.9) | copy-start | bytes 1540
  137.2 3.8 %copy-start.1 = (bf16[2048,128]{1,0:T(8,128)(2,1)S(1)}, bf16[2048,128]{1,0:T(8,128)(2,1)}, u32[]{:S(2)}) copy-start(bf16[2048,128]{1,0:T(8,128)(2,1)} %get-tuple-element.250) | copy-start | bytes 1572868 | tf_op jit(solution)/shard_map/while
  139.0 1.9 copy-start
  146.1 3.8 %copy-start.1 = (bf16[2048,128]{1,0:T(8,128)(2,1)S(1)}, bf16[2048,128]{1,0:T(8,128)(2,1)}, u32[]{:S(2)}) copy-start(bf16[2048,128]{1,0:T(8,128)(2,1)} %get-tuple-element.250) | copy-start | bytes 1572868 | tf_op jit(solution)/shard_map/while
  148.0 1.9 copy-start
  155.1 3.8 %copy-start.1 = (bf16[2048,128]{1,0:T(8,128)(2,1)S(1)}, bf16[2048,128]{1,0:T(8,128)(2,1)}, u32[]{:S(2)}) copy-start(bf16[2048,128]{1,0:T(8,128)(2,1)} %get-tuple-element.250) | copy-start | bytes 1572868 | tf_op jit(solution)/shard_map/while
  157.0 1.9 copy-start
  164.1 3.8 %copy-start.1 = (bf16[2048,128]{1,0:T(8,128)(2,1)S(1)}, bf16[2048,128]{1,0:T(8,128)(2,1)}, u32[]{:S(2)}) copy-start(bf16[2048,128]{1,0:T(8,128)(2,1)} %get-tuple-element.250) | copy-start | bytes 1572868 | tf_op jit(solution)/shard_map/while
  166.0 1.9 copy-start
  173.1 3.8 %copy-start.1 = (bf16[2048,128]{1,0:T(8,128)(2,1)S(1)}, bf16[2048,128]{1,0:T(8,128)(2,1)}, u32[]{:S(2)}) copy-start(bf16[2048,128]{1,0:T(8,128)(2,1)} %get-tuple-element.250) | copy-start | bytes 1572868 | tf_op jit(solution)/shard_map/while
  175.0 1.9 copy-start
  182.1 3.8 %copy-start.1 = (bf16[2048,128]{1,0:T(8,128)(2,1)S(1)}, bf16[2048,128]{1,0:T(8,128)(2,1)}, u32[]{:S(2)}) copy-start(bf16[2048,128]{1,0:T(8,128)(2,1)} %get-tuple-element.250) | copy-start | bytes 1572868 | tf_op jit(solution)/shard_map/while
  184.0 1.9 copy-start
  191.2 3.8 %copy-start.1 = (bf16[2048,128]{1,0:T(8,128)(2,1)S(1)}, bf16[2048,128]{1,0:T(8,128)(2,1)}, u32[]{:S(2)}) copy-start(bf16[2048,128]{1,0:T(8,128)(2,1)} %get-tuple-element.250) | copy-start | bytes 1572868 | tf_op jit(solution)/shard_map/while
  193.0 1.9 copy-start
  200.2 3.8 %copy-start.1 = (bf16[2048,128]{1,0:T(8,128)(2,1)S(1)}, bf16[2048,128]{1,0:T(8,128)(2,1)}, u32[]{:S(2)}) copy-start(bf16[2048,128]{1,0:T(8,128)(2,1)} %get-tuple-element.250) | copy-start | bytes 1572868 | tf_op jit(solution)/shard_map/while
  202.0 1.9 copy-start
  209.2 1.0 copy-start.2
  210.2 139.0 %reduce-scatter.3.cloned.1.call-start = ((), (), s32[]{:S(2)}) async-start(), calls=%async_computation.2 | async-start | bytes 2228224 | tf_op jit(solution)/shard_map/reduce_scatter | solution.py:65
Sparse Core Ops, SparseCore 0:
  210.3 73.8 reduce-scatter.4
  287.2 61.9 reduce-scatter.2
where the time goes:
time: 359 us; the launch traced here: 356 us
  waiting for transfers between devices  139 us (39%)
  blocking collectives  107 us (30%)
  matrix products  71.5 us (20%)
  local copies, waits for them, and re-layouts  17.5 us (5%)
  between operations  14.1 us (4%)
  other arithmetic  6.62 us (2%)
    reduce_scatter x1, waiting for transfers between devices, shards(): lax.psum_scatter(doc_total, 'query', scatter_dimension=0, tiled=True)  73.3 us
    reduce_scatter x1, waiting for transfers between devices, shards(): lax.psum_scatter(query_terms, 'tok', scatter_dimension=0, tiled=True)  65 us
    pmax x1, blocking collectives, shards(): top_all = lax.pmax(row_tops, 'tok')  53.6 us
    psum x1, blocking collectives, shards(): total_all = lax.psum(row_totals * jnp.exp(row_tops - top_all), 'tok')  52.9 us
    dot_general x16, matrix products, score_rows(): lax.dot_general(q_rows, doc_rows, (((1,), (1,)), ((), ())), preferred_ele...  30.2 us
    dot_general x8, matrix products, backward_both(): lax.dot_general(scaled, q_rows, (((0,), (0,)), ((), ())), preferred_eleme...  28.9 us
    while x32, local copies, waits for them, and re-layouts  15.2 us
    dot_general x8, matrix products, backward_both(): jnp.dot(weights_low, documents, preferred_element_type=jnp.float32)  12.4 us
  transfers between devices with their start and end apart: 2, of which 2 were waited for; matrix products, arithmetic and copies ran while one was open for 0% of the time, Pallas kernels for 0%

commit v1 on v0

v1 whole, which is shorter than its diff:
```python
import functools

import jax
import jax.numpy as jnp
from jax import lax
from jax.experimental import pallas as pl
from jax.experimental.pallas import tpu as pltpu
from jax.sharding import PartitionSpec as P

QLEN = 32
inv_temp = 2.0
LOG2E = 1.4426950408889634
SCALE = inv_temp * LOG2E

MESH = pl.DeviceIdType.MESH
F32 = jnp.float32
BF16 = jnp.bfloat16

BLK = 256
NBLK = 16
NDBLK = 8
DIM = 128
CHUNK = 256
NCHUNK = 8


def block_of(slot):
    half, rest = slot // 8, lax.rem(slot, 8)
    y, core = rest // 2, lax.rem(rest, 2)
    return 4 * y + 2 * lax.rem(half + y, 2) + core


def kernel(
    q_ref, d_ref, cot_ref, gq_ref, gd_ref,
    s_ref, u_ref, dc_ref, dt_ref, lse_mine, lse_all, lse_ref,
    pair_out, pair_in, part, q_out, q_in, d_out, d_in, d_own,
    lse_ss, lse_rs, pair_ss, pair_rs, q_ss, q_rs, d_ss, d_rs,
):
    qi, ti = lax.axis_index("query"), lax.axis_index("tok")
    x0, zh0 = qi // 2, lax.rem(qi, 2)
    y0, z0, core = ti // 4, lax.rem(ti // 2, 2), lax.rem(ti, 2)

    barrier = pltpu.get_barrier_semaphore()
    for k in range(1, 16):
        pl.semaphore_signal(barrier, inc=1, device_id=(qi, lax.rem(ti + k, 16)), device_id_type=MESH)
    for k in range(1, 8):
        pl.semaphore_signal(barrier, inc=1, device_id=(lax.rem(qi + k, 8), ti), device_id_type=MESH)

    for c in range(NCHUNK):
        rows = slice(c * CHUNK, (c + 1) * CHUNK)
        scaled = d_ref[rows, :].astype(F32) * SCALE
        high = scaled.astype(BF16)
        dc_ref[rows, 0:DIM] = high
        dc_ref[rows, DIM : 2 * DIM] = (scaled - high.astype(F32)).astype(BF16)

    def q_pair(slot):
        rows = q_ref[pl.ds(pl.multiple_of(block_of(slot) * BLK, BLK), BLK), :]
        return jnp.concatenate([rows, rows], axis=1)

    def score_chunk(slot, c, q2):
        rows = slice(c * CHUNK, (c + 1) * CHUNK)
        s = lax.dot_general(dc_ref[rows, :], q2, (((1,), (1,)), ((), ())), preferred_element_type=F32)
        s_ref[slot, rows, :] = s
        return jnp.max(s.reshape(CHUNK // 8, 8, BLK), axis=0)

    def exp_chunk(slot, c, top, total):
        e = jnp.exp2(s_ref[slot, slice(c * CHUNK, (c + 1) * CHUNK), :] - top)
        return total + jnp.sum(e.reshape(CHUNK // 8, 8, BLK), axis=0)

    def local_lse(half, row, top, total):
        lse_mine[half, pl.ds(row, 1), :] = top + jnp.log2(jnp.sum(total, axis=0, keepdims=True))

    def scores_of(slot):
        q2 = q_pair(slot)
        tops = score_chunk(slot, 0, q2)
        for c in range(1, NCHUNK):
            tops = jnp.maximum(tops, score_chunk(slot, c, q2))
        return tops

    def step_a(half):
        def body(slot, tops):
            cols = pl.ds(pl.multiple_of(slot * DIM, DIM), DIM)
            dt_ref[:, cols] = d_ref[cols, :].T
            top = jnp.max(tops, axis=0, keepdims=True)
            total = jnp.zeros((8, BLK), F32)
            q2 = q_pair(slot + 1)
            new = None
            for c in range(NCHUNK):
                total = exp_chunk(slot, c, top, total)
                t = score_chunk(slot + 1, c, q2)
                new = t if new is None else jnp.maximum(new, t)
            local_lse(half, slot - 8 * half, top, total)
            return new

        return body

    def lse_copy(half, k):
        return pltpu.make_async_remote_copy(
            src_ref=lse_mine.at[half], dst_ref=lse_all.at[half, k - 1],
            send_sem=lse_ss.at[half, k - 1], recv_sem=lse_rs.at[half, k - 1],
            device_id=(qi, lax.rem(ti + k, 16)), device_id_type=MESH,
        )

    tops = lax.fori_loop(0, 8, step_a(0), scores_of(0))
    pl.semaphore_wait(barrier, 22)
    for k in range(1, 16):
        lse_copy(0, k).start()
    tops = lax.fori_loop(8, 15, step_a(1), tops)
    cols = slice(15 * DIM, 16 * DIM)
    dt_ref[:, cols] = d_ref[cols, :].T
    top = jnp.max(tops, axis=0, keepdims=True)
    total = jnp.zeros((8, BLK), F32)
    for c in range(NCHUNK):
        total = exp_chunk(15, c, top, total)
    local_lse(1, 7, top, total)
    for k in range(1, 16):
        lse_copy(1, k).start()

    lane_query = lax.broadcasted_iota(jnp.int32, (1, BLK), 1) // QLEN

    def weights_of(block):
        w = jnp.zeros((1, BLK), F32)
        for g in range(BLK // QLEN):
            w = jnp.where(lane_query == g, cot_ref[block * (BLK // QLEN) + g], w)
        return w

    def probs_of(slot):
        lse = lse_ref[pl.ds(slot, 1), :]
        w = weights_of(block_of(slot))
        acc = jnp.zeros((DIM, BLK), F32)
        for c in range(NCHUNK):
            rows = slice(c * CHUNK, (c + 1) * CHUNK)
            p = jnp.exp2(s_ref[slot, rows, :] - lse)
            u_ref[slot, rows, :] = (w * p).astype(BF16)
            acc = acc + jnp.dot(dt_ref[:, rows], p.astype(BF16), preferred_element_type=F32)
        return (w * acc).T

    def pair_copy(st):
        return pltpu.make_async_remote_copy(
            src_ref=pair_out.at[st], dst_ref=pair_in.at[st],
            send_sem=pair_ss.at[st], recv_sem=pair_rs.at[st],
            device_id=(qi, ti + 1 - 2 * core), device_id_type=MESH,
        )

    def target(st):
        half, k = st // 4, lax.rem(st, 4)
        y = lax.rem(y0 + 1 + k, 4)
        return k, y, lax.rem(half + y, 2)

    def q_copy(st):
        k, y, z = target(st)
        slot = 2 * k + z0
        return pltpu.make_async_remote_copy(
            src_ref=q_out.at[st], dst_ref=q_in.at[slot],
            send_sem=q_ss.at[st], recv_sem=q_rs.at[slot],
            device_id=(qi, 4 * y + 2 * z + core), device_id_type=MESH,
        )

    def finish(st):
        pair_copy(st).wait_recv()
        both = part[st] + pair_in[st]
        part[st] = both
        q_out[st] = both.astype(BF16)

    def is_remote(st):
        k, y, z = target(st)
        return jnp.logical_or(k != 3, z != z0)

    def send(st):
        @pl.when(is_remote(st))
        def _():
            q_copy(st).start()

    def step_b(st, _):
        _, y, _ = target(st)
        base = 8 * (st // 4) + 2 * y
        pair_out[st] = probs_of(base + 1 - core)

        @pl.when(st > 0)
        def _():
            finish(st - 1)

        part[st] = probs_of(base + core)
        pair_copy(st).start()

        @pl.when(st > 0)
        def _():
            send(st - 1)

        return 0

    for half in range(2):
        for k in range(1, 16):
            lse_copy(half, k).wait_recv()
        top = lse_mine[half]
        for k in range(15):
            top = jnp.maximum(top, lse_all[half, k])
        total = jnp.exp2(lse_mine[half] - top)
        for k in range(15):
            total = total + jnp.exp2(lse_all[half, k] - top)
        lse_ref[8 * half : 8 * half + 8, :] = top + jnp.log2(total)
        lax.fori_loop(4 * half, 4 * half + 4, step_b, 0)

    def d_copy(m):
        x = lax.rem(x0 + lax.rem(m, 4) + 1, 4)
        zh = lax.rem(zh0 + 1 + m // 4, 2)
        return pltpu.make_async_remote_copy(
            src_ref=d_out.at[m], dst_ref=d_in.at[m],
            send_sem=d_ss.at[m], recv_sem=d_rs.at[m],
            device_id=(2 * x + zh, ti), device_id_type=MESH,
        )

    def docs_of(m):
        x = lax.rem(x0 + lax.rem(m, 4) + 1, 4)
        zh = lax.rem(zh0 + 1 + m // 4, 2)
        rows = pl.ds(pl.multiple_of((2 * x + zh) * BLK, BLK), BLK)
        acc = jnp.zeros((BLK, DIM), F32)
        for slot in range(NBLK):
            half, y, cb = slot // 8, (slot % 8) // 2, slot % 2
            blk = 4 * y + 2 * ((half + y) % 2) + cb
            acc = acc + jnp.dot(
                u_ref[slot, rows, :], q_ref[blk * BLK : (blk + 1) * BLK, :], preferred_element_type=F32
            )
        return acc

    def step_c(m, _):
        d_out[m] = docs_of(m).astype(BF16)
        d_copy(m).start()
        return 0

    finish(7)
    send(7)
    lax.fori_loop(0, 7, step_c, 0)
    d_own[...] = docs_of(7)

    mine = jnp.where(lax.rem(y0 + z0, 2) == 0, 3, 7)
    gq_ref[...] = part[mine]
    for k in range(4):
        for z in range(2):
            slot = 2 * k + z

            def add(slot=slot):
                q_copy_in = pltpu.make_async_remote_copy(
                    src_ref=q_out.at[0], dst_ref=q_in.at[slot],
                    send_sem=q_ss.at[0], recv_sem=q_rs.at[slot],
                    device_id=(qi, lax.rem(ti + 2, 16)), device_id_type=MESH,
                )
                q_copy_in.wait_recv()
                gq_ref[...] += q_in[slot].astype(F32)

            if k < 3:
                add()
            else:
                pl.when(z != z0)(add)
    total = d_own[...]
    for m in range(7):
        d_copy(m).wait_recv()
        total = total + d_in[m].astype(F32)
    gd_ref[0] = total

    for half in range(2):
        for k in range(1, 16):
            lse_copy(half, k).wait_send()
    for st in range(8):
        pair_copy(st).wait_send()

        @pl.when(is_remote(st))
        def _():
            q_copy(st).wait_send()

    for m in range(7):
        d_copy(m).wait_send()


def shards(queries, documents, cotangent):
    vmem = pl.BlockSpec(memory_space=pltpu.VMEM)
    dma = pltpu.SemaphoreType.DMA
    n_docs = documents.shape[0]
    return pl.pallas_call(
        kernel,
        out_shape=(
            jax.ShapeDtypeStruct((BLK, DIM), F32),
            jax.ShapeDtypeStruct((1, BLK, DIM), F32),
        ),
        in_specs=[vmem, vmem, pl.BlockSpec(memory_space=pltpu.SMEM)],
        out_specs=(vmem, vmem),
        scratch_shapes=[
            pltpu.VMEM((NBLK, n_docs, BLK), F32),
            pltpu.VMEM((NBLK, n_docs, BLK), BF16),
            pltpu.VMEM((n_docs, 2 * DIM), BF16),
            pltpu.VMEM((DIM, n_docs), BF16),
            pltpu.VMEM((2, 8, BLK), F32),
            pltpu.VMEM((2, 15, 8, BLK), F32),
            pltpu.VMEM((NBLK, BLK), F32),
            pltpu.VMEM((8, BLK, DIM), F32),
            pltpu.VMEM((8, BLK, DIM), F32),
            pltpu.VMEM((8, BLK, DIM), F32),
            pltpu.VMEM((8, BLK, DIM), BF16),
            pltpu.VMEM((8, BLK, DIM), BF16),
            pltpu.VMEM((7, BLK, DIM), BF16),
            pltpu.VMEM((7, BLK, DIM), BF16),
            pltpu.VMEM((BLK, DIM), F32),
            dma((2, 15)), dma((2, 15)), dma((8,)), dma((8,)),
            dma((8,)), dma((8,)), dma((7,)), dma((7,)),
        ],
        compiler_params=pltpu.CompilerParams(
            collective_id=0, has_side_effects=True, vmem_limit_bytes=67043328
        ),
    )(queries, documents, cotangent)


def solution(mesh):
    placed = (P("query", None), P("tok", None), P("query"))
    return jax.shard_map(
        shards,
        mesh=mesh,
        in_specs=placed,
        out_specs=(P(("query", "tok"), None), P("tok", "query", None)),
        check_vma=False,
    )
```

time: 359 us -> 47.1 us (0.13)
  waiting for transfers between devices: 139 us -> 0 us
  blocking collectives: 107 us -> 0 us
  matrix products: 71.5 us -> 0 us
  Pallas kernels: 0 us -> 44 us
  local copies, waits for them, and re-layouts: 17.5 us -> 2.26 us
  between operations: 14.1 us -> 0.65 us
  other arithmetic: 6.62 us -> 0 us
    reduce_scatter x2 -> x0, waiting for transfers between devices: 138 us -> none  [the longest x1 73.3 us: shards(): lax.psum_scatter(doc_total, 'query', scatter_dimension=0, tiled=True)]
    dot_general x32 -> x0, matrix products: 71.5 us -> none  [the longest x16 30.2 us: score_rows(): lax.dot_general(q_rows, doc_rows, (((1,), (1,)), ((), ())), preferred_ele...]
    pmax x1 -> x0, blocking collectives: 53.6 us -> none  [shards(): top_all = lax.pmax(row_tops, 'tok')]
    psum x1 -> x0, blocking collectives: 52.9 us -> none  [shards(): total_all = lax.psum(row_totals * jnp.exp(row_tops - top_all), 'tok')]
    pallas_call x0 -> x1, Pallas kernels: none -> 44 us  [shards(): pl.pallas_call(kernel, out_shape=(jax.ShapeDtypeStruct((BLK, DIM), F32),...]
    while x32 -> x0, local copies, waits for them, and re-layouts: 15.2 us -> none
    reduce_sum x8 -> x0, other arithmetic: 6.59 us -> none  [local_stats(): row_total = jnp.sum(jnp.exp(scores - row_top[:, None]), axis=1)]
  transfers between devices with their start and end apart: 2 -> 0, of which waited for: 2 -> 0; matrix products, arithmetic and copies ran while one was open for 0% -> 0% of each run, Pallas kernels for 0% -> 0%
where the time goes in v1:
time: 47.1 us; the launch traced here: 46.9 us
  Pallas kernels  44 us (93%)
  local copies, waits for them, and re-layouts  2.26 us (5%)
  between operations  0.65 us (1%)
    pallas_call x1, Pallas kernels, shards(): pl.pallas_call(kernel, out_shape=(jax.ShapeDtypeStruct((BLK, DIM), F32),...  44 us
    unnamed x4, local copies, waits for them, and re-layouts  2.26 us

profile of v1, /device:TPU:1, one launch (start us, length us, event | category | flops | bytes accessed | tf_op | source)
XLA Modules:
  0.0 46.9 jit_solution(11774702409025441501)
XLA Ops:
  0.6 44.0 %shard_map.50 = (f32[256,128]{1,0:T(8,128)}, f32[1,256,128]{2,1,0:T(8,128)}) custom-call(bf16[4096,128]{1,0:T(8,128)(2,1)} %q_ref.1, bf16[2048,128]{1,0:T(8,128)(2,1)} %d_ref.1, f32[128]{0:T(128)} %cot_ref.1), custom_call_target="tpu_custom_call" | custom-call | tf_op jit(solution)/shard_map/pallas_call | solution.py:279
  44.6 0.0 copy-start
  44.6 1.6 %copy.7 = f32[256,128]{1,0:T(8,128)} copy(f32[256,128]{1,0:T(8,128)} %get-tuple-element.4) | data formatting | bytes 262144
  46.2 0.0 copy-done
  46.2 0.7 %copy.8 = f32[1,256,128]{2,1,0:T(8,128)} copy(f32[1,256,128]{2,1,0:T(8,128)S(1)} %copy-done) | data formatting | bytes 262144
Async XLA Ops:
  44.6 1.6 %copy-start = (f32[1,256,128]{2,1,0:T(8,128)S(1)}, f32[1,256,128]{2,1,0:T(8,128)}, u32[]{:S(2)}) copy-start(f32[1,256,128]{2,1,0:T(8,128)} %get-tuple-element.5) | copy-start | bytes 393220

commit v2 on v1

--- a/solution.py
+++ b/solution.py
@@ -22,6 +22,7 @@
 DIM = 128
 CHUNK = 256
 NCHUNK = 8
+SUBROWS = 16
 
 
 def block_of(slot):
@@ -57,40 +58,49 @@
         rows = q_ref[pl.ds(pl.multiple_of(block_of(slot) * BLK, BLK), BLK), :]
         return jnp.concatenate([rows, rows], axis=1)
 
-    def score_chunk(slot, c, q2):
+    def score_chunk(slot, c, q2, tops):
         rows = slice(c * CHUNK, (c + 1) * CHUNK)
         s = lax.dot_general(dc_ref[rows, :], q2, (((1,), (1,)), ((), ())), preferred_element_type=F32)
         s_ref[slot, rows, :] = s
-        return jnp.max(s.reshape(CHUNK // 8, 8, BLK), axis=0)
+        for i in range(0, CHUNK, SUBROWS):
+            part_s = s[i : i + SUBROWS]
+            tops = part_s if tops is None else jnp.maximum(tops, part_s)
+        return tops
 
     def exp_chunk(slot, c, top, total):
-        e = jnp.exp2(s_ref[slot, slice(c * CHUNK, (c + 1) * CHUNK), :] - top)
-        return total + jnp.sum(e.reshape(CHUNK // 8, 8, BLK), axis=0)
+        for i in range(c * CHUNK, (c + 1) * CHUNK, SUBROWS):
+            e = jnp.exp2(s_ref[slot, i : i + SUBROWS, :] - top)
+            total = e if total is None else total + e
+        return total
 
     def local_lse(half, row, top, total):
         lse_mine[half, pl.ds(row, 1), :] = top + jnp.log2(jnp.sum(total, axis=0, keepdims=True))
 
     def scores_of(slot):
         q2 = q_pair(slot)
-        tops = score_chunk(slot, 0, q2)
-        for c in range(1, NCHUNK):
-            tops = jnp.maximum(tops, score_chunk(slot, c, q2))
-        return tops
+        tops = None
+        for c in range(NCHUNK):
+            tops = score_chunk(slot, c, q2, tops)
+        return jnp.max(tops, axis=0, keepdims=True)
+
+    def turn(i):
+        cols = pl.ds(pl.multiple_of(i * 2 * DIM, 2 * DIM), 2 * DIM)
+        dt_ref[:, cols] = d_ref[cols, :].T
 
     def step_a(half):
-        def body(slot, tops):
-            cols = pl.ds(pl.multiple_of(slot * DIM, DIM), DIM)
-            dt_ref[:, cols] = d_ref[cols, :].T
-            top = jnp.max(tops, axis=0, keepdims=True)
-            total = jnp.zeros((8, BLK), F32)
-            q2 = q_pair(slot + 1)
-            new = None
-            for c in range(NCHUNK):
-                total = exp_chunk(slot, c, top, total)
-                t = score_chunk(slot + 1, c, q2)
-                new = t if new is None else jnp.maximum(new, t)
-            local_lse(half, slot - 8 * half, top, total)
-            return new
+        def body(i, tops):
+            turn(i)
+            new = []
+            for k in range(2):
+                slot = 2 * i + k
+                q2 = q_pair(slot + 2)
+                total = fresh = None
+                for c in range(NCHUNK):
+                    total = exp_chunk(slot, c, tops[k], total)
+                    fresh = score_chunk(slot + 2, c, q2, fresh)
+                local_lse(half, slot - 8 * half, tops[k], total)
+                new.append(jnp.max(fresh, axis=0, keepdims=True))
+            return tuple(new)
 
         return body
 
@@ -101,18 +111,17 @@
             device_id=(qi, lax.rem(ti + k, 16)), device_id_type=MESH,
         )
 
-    tops = lax.fori_loop(0, 8, step_a(0), scores_of(0))
+    tops = lax.fori_loop(0, 4, step_a(0), (scores_of(0), scores_of(1)))
     pl.semaphore_wait(barrier, 22)
     for k in range(1, 16):
         lse_copy(0, k).start()
-    tops = lax.fori_loop(8, 15, step_a(1), tops)
-    cols = slice(15 * DIM, 16 * DIM)
-    dt_ref[:, cols] = d_ref[cols, :].T
-    top = jnp.max(tops, axis=0, keepdims=True)
-    total = jnp.zeros((8, BLK), F32)
-    for c in range(NCHUNK):
-        total = exp_chunk(15, c, top, total)
-    local_lse(1, 7, top, total)
+    tops = lax.fori_loop(4, 7, step_a(1), tops)
+    turn(7)
+    for k in range(2):
+        total = None
+        for c in range(NCHUNK):
+            total = exp_chunk(14 + k, c, tops[k], total)
+        local_lse(1, 6 + k, tops[k], total)
     for k in range(1, 16):
         lse_copy(1, k).start()
 
@@ -171,21 +180,21 @@
         def _():
             q_copy(st).start()
 
-    def step_b(st, _):
-        _, y, _ = target(st)
-        base = 8 * (st // 4) + 2 * y
-        pair_out[st] = probs_of(base + 1 - core)
-
-        @pl.when(st > 0)
+    def step_b(i, _):
+        for st in (2 * i, 2 * i + 1):
+            _, y, _ = target(st)
+            base = 8 * (st // 4) + 2 * y
+            pair_out[st] = probs_of(base + 1 - core)
+            part[st] = probs_of(base + core)
+        for st in (2 * i, 2 * i + 1):
+            pair_copy(st).start()
+
+        @pl.when(i > 0)
         def _():
-            finish(st - 1)
-
-        part[st] = probs_of(base + core)
-        pair_copy(st).start()
-
-        @pl.when(st > 0)
-        def _():
-            send(st - 1)
+            for st in (2 * i - 2, 2 * i - 1):
+                finish(st)
+            for st in (2 * i - 2, 2 * i - 1):
+                send(st)
 
         return 0
 
@@ -199,7 +208,7 @@
         for k in range(15):
             total = total + jnp.exp2(lse_all[half, k] - top)
         lse_ref[8 * half : 8 * half + 8, :] = top + jnp.log2(total)
-        lax.fori_loop(4 * half, 4 * half + 4, step_b, 0)
+        lax.fori_loop(2 * half, 2 * half + 2, step_b, 0)
 
     def d_copy(m):
         x = lax.rem(x0 + lax.rem(m, 4) + 1, 4)
@@ -228,9 +237,12 @@
         d_copy(m).start()
         return 0
 
-    finish(7)
-    send(7)
-    lax.fori_loop(0, 7, step_c, 0)
+    lax.fori_loop(0, 1, step_c, 0)
+    for st in (6, 7):
+        finish(st)
+    for st in (6, 7):
+        send(st)
+    lax.fori_loop(1, 7, step_c, 0)
     d_own[...] = docs_of(7)
 
     mine = jnp.where(lax.rem(y0 + z0, 2) == 0, 3, 7)

time: 47.1 us -> 40.8 us (0.87)
  Pallas kernels: 44 us -> 37.7 us
    pallas_call x1, Pallas kernels: 44 us -> 37.7 us  [shards(): pl.pallas_call(kernel, out_shape=(jax.ShapeDtypeStruct((BLK, DIM), F32),...]
where the time goes in v2:
time: 40.8 us; the launch traced here: 40.7 us
  Pallas kernels  37.7 us (92%)
  local copies, waits for them, and re-layouts  2.26 us (6%)
  between operations  0.65 us (2%)
    pallas_call x1, Pallas kernels, shards(): pl.pallas_call(kernel, out_shape=(jax.ShapeDtypeStruct((BLK, DIM), F32),...  37.7 us
    unnamed x4, local copies, waits for them, and re-layouts  2.26 us

profile of v2, /device:TPU:1, one launch (start us, length us, event | category | flops | bytes accessed | tf_op | source)
XLA Modules:
  0.0 40.7 jit_solution(8439527144049348750)
XLA Ops:
  0.6 37.7 %shard_map.50 = (f32[256,128]{1,0:T(8,128)}, f32[1,256,128]{2,1,0:T(8,128)}) custom-call(bf16[4096,128]{1,0:T(8,128)(2,1)} %q_ref.1, bf16[2048,128]{1,0:T(8,128)(2,1)} %d_ref.1, f32[128]{0:T(128)} %cot_ref.1), custom_call_target="tpu_custom_call" | custom-call | tf_op jit(solution)/shard_map/pallas_call | solution.py:291
  38.4 0.0 copy-start
  38.4 1.6 %copy.7 = f32[256,128]{1,0:T(8,128)} copy(f32[256,128]{1,0:T(8,128)} %get-tuple-element.4) | data formatting | bytes 262144
  40.0 0.0 copy-done
  40.0 0.7 %copy.8 = f32[1,256,128]{2,1,0:T(8,128)} copy(f32[1,256,128]{2,1,0:T(8,128)S(1)} %copy-done) | data formatting | bytes 262144
Async XLA Ops:
  38.4 1.6 %copy-start = (f32[1,256,128]{2,1,0:T(8,128)S(1)}, f32[1,256,128]{2,1,0:T(8,128)}, u32[]{:S(2)}) copy-start(f32[1,256,128]{2,1,0:T(8,128)} %get-tuple-element.5) | copy-start | bytes 393220

commit v3 on v2

v3 whole, which is shorter than its diff:
```python
import functools

import jax
import jax.numpy as jnp
from jax import lax
from jax.experimental import pallas as pl
from jax.experimental.pallas import tpu as pltpu
from jax.sharding import PartitionSpec as P

QLEN = 32
inv_temp = 2.0
LOG2E = 1.4426950408889634
SCALE = inv_temp * LOG2E

MESH = pl.DeviceIdType.MESH
F32 = jnp.float32
BF16 = jnp.bfloat16

BLK = 256
NBLK = 16
NDBLK = 8
DIM = 128
CHUNK = 256
NCHUNK = 8
SUBROWS = 16


def static_block(slot):
    half, y, core = slot // 8, (slot % 8) // 2, slot % 2
    return 4 * y + 2 * ((half + y) % 2) + core


def block_of(slot):
    half, rest = slot // 8, lax.rem(slot, 8)
    y, core = rest // 2, lax.rem(rest, 2)
    return 4 * y + 2 * lax.rem(half + y, 2) + core


def kernel(
    q_ref, d_ref, cot_ref, gq_ref, gd_ref,
    s_ref, dc_ref, dt_ref, w_ref, lse_mine, lse_all, lse_ref,
    pair_out, pair_in, part, q_out, q_in, d_part, d_out, d_in,
    lse_ss, lse_rs, pair_ss, pair_rs, q_ss, q_rs, d_ss, d_rs,
):
    qi, ti = lax.axis_index("query"), lax.axis_index("tok")
    x0, zh0 = qi // 2, lax.rem(qi, 2)
    y0, z0, core = ti // 4, lax.rem(ti // 2, 2), lax.rem(ti, 2)

    barrier = pltpu.get_barrier_semaphore()
    for k in range(1, 16):
        pl.semaphore_signal(barrier, inc=1, device_id=(qi, lax.rem(ti + k, 16)), device_id_type=MESH)
    for k in range(1, 8):
        pl.semaphore_signal(barrier, inc=1, device_id=(lax.rem(qi + k, 8), ti), device_id_type=MESH)

    for c in range(NCHUNK):
        rows = slice(c * CHUNK, (c + 1) * CHUNK)
        scaled = d_ref[rows, :].astype(F32) * SCALE
        high = scaled.astype(BF16)
        dc_ref[rows, 0:DIM] = high
        dc_ref[rows, DIM : 2 * DIM] = (scaled - high.astype(F32)).astype(BF16)
        dt_ref[:, rows] = d_ref[rows, :].T

    def target(st):
        half, k = st // 4, lax.rem(st, 4)
        y = lax.rem(y0 + 1 + k, 4)
        return k, y, lax.rem(half + y, 2)

    def slots_of(st):
        _, y, _ = target(st)
        base = 8 * (st // 4) + 2 * y
        return base + 1 - core, base + core

    def q_pair(slot):
        rows = q_ref[pl.ds(pl.multiple_of(block_of(slot) * BLK, BLK), BLK), :]
        return jnp.concatenate([rows, rows], axis=1)

    def score_chunk(slot, c, q2, tops):
        rows = slice(c * CHUNK, (c + 1) * CHUNK)
        s = lax.dot_general(dc_ref[rows, :], q2, (((1,), (1,)), ((), ())), preferred_element_type=F32)
        s_ref[slot, rows, :] = s
        for i in range(0, CHUNK, SUBROWS):
            part_s = s[i : i + SUBROWS]
            tops = part_s if tops is None else jnp.maximum(tops, part_s)
        return tops

    def scores_of(slot):
        q2 = q_pair(slot)
        tops = None
        for c in range(NCHUNK):
            tops = score_chunk(slot, c, q2, tops)
        return jnp.max(tops, axis=0, keepdims=True)

    def step_a(st, tops, half, more):
        new = []
        slots = slots_of(st)
        following = slots_of(st + 1)
        for k in range(2):
            slot = slots[k]
            q2 = q_pair(following[k]) if more else None
            total = fresh = None
            acc = jnp.zeros((DIM, BLK), F32)
            for c in range(NCHUNK):
                rows = slice(c * CHUNK, (c + 1) * CHUNK)
                e = jnp.exp2(s_ref[slot, rows, :] - tops[k])
                for i in range(0, CHUNK, SUBROWS):
                    part_e = e[i : i + SUBROWS]
                    total = part_e if total is None else total + part_e
                acc = acc + jnp.dot(dt_ref[:, rows], e.astype(BF16), preferred_element_type=F32)
                if more:
                    fresh = score_chunk(following[k], c, q2, fresh)
            total = jnp.sum(total, axis=0, keepdims=True)
            lse = tops[k] + jnp.log2(total)
            lse_mine[half, pl.ds(slot - 8 * half, 1), :] = lse
            mean = acc * (1.0 / total)
            if k == 0:
                pair_out[st, 0:DIM, :] = mean
                pair_out[st, DIM : DIM + 8, :] = jnp.broadcast_to(lse, (8, BLK))
            else:
                part[st] = mean
            if more:
                new.append(jnp.max(fresh, axis=0, keepdims=True))
        return tuple(new)

    def lse_copy(half, k):
        return pltpu.make_async_remote_copy(
            src_ref=lse_mine.at[half], dst_ref=lse_all.at[half, k - 1],
            send_sem=lse_ss.at[half, k - 1], recv_sem=lse_rs.at[half, k - 1],
            device_id=(qi, lax.rem(ti + k, 16)), device_id_type=MESH,
        )

    def pair_copy(st):
        return pltpu.make_async_remote_copy(
            src_ref=pair_out.at[st], dst_ref=pair_in.at[st],
            send_sem=pair_ss.at[st], recv_sem=pair_rs.at[st],
            device_id=(qi, ti + 1 - 2 * core), device_id_type=MESH,
        )

    def q_copy(st):
        k, y, z = target(st)
        slot = 2 * k + z0
        return pltpu.make_async_remote_copy(
            src_ref=q_out.at[st], dst_ref=q_in.at[slot],
            send_sem=q_ss.at[st], recv_sem=q_rs.at[slot],
            device_id=(qi, 4 * y + 2 * z + core), device_id_type=MESH,
        )

    def finish(st, half):
        pair_copy(st).wait_recv()
        mine = lse_mine[half, pl.ds(slots_of(st)[1] - 8 * half, 1), :]
        theirs = pair_in[st, DIM : DIM + 1, :]
        top = jnp.maximum(mine, theirs)
        a, b = jnp.exp2(mine - top), jnp.exp2(theirs - top)
        scale = 1.0 / (a + b)
        both = part[st] * (a * scale) + pair_in[st, 0:DIM, :] * (b * scale)
        part[st] = both
        q_out[st] = both.astype(BF16)

    def is_remote(st):
        k, _, z = target(st)
        return jnp.logical_or(k != 3, z != z0)

    def send(st):
        @pl.when(is_remote(st))
        def _():
            q_copy(st).start()

    first = slots_of(0)
    tops = lax.fori_loop(
        0, 4, lambda st, tops: step_a(st, tops, 0, True), (scores_of(first[0]), scores_of(first[1]))
    )
    pl.semaphore_wait(barrier, 22)
    for k in range(1, 16):
        lse_copy(0, k).start()
    for st in range(4):
        pair_copy(st).start()

    def second(st, tops):
        tops = step_a(st, tops, 1, True)
        finish(st - 4, 0)
        pair_copy(st).start()
        send(st - 4)
        return tops

    tops = lax.fori_loop(4, 7, second, tops)
    step_a(7, tops, 1, False)
    for k in range(1, 16):
        lse_copy(1, k).start()
    pair_copy(7).start()

    lane_query = lax.broadcasted_iota(jnp.int32, (1, BLK), 1) // QLEN
    for slot in range(NBLK):
        w = jnp.zeros((1, BLK), F32)
        for g in range(BLK // QLEN):
            w = jnp.where(lane_query == g, cot_ref[static_block(slot) * (BLK // QLEN) + g], w)
        w_ref[slot : slot + 1, :] = w
    finish(3, 0)
    send(3)
    for st in range(4, 7):
        finish(st, 1)
        send(st)

    def global_lse(half):
        for k in range(1, 16):
            lse_copy(half, k).wait_recv()
        top = lse_mine[half]
        for k in range(15):
            top = jnp.maximum(top, lse_all[half, k])
        total = jnp.exp2(lse_mine[half] - top)
        for k in range(15):
            total = total + jnp.exp2(lse_all[half, k] - top)
        lse_ref[8 * half : 8 * half + 8, :] = top + jnp.log2(total)

    def d_target(m):
        x = lax.rem(x0 + lax.rem(m, 4) + 1, 4)
        zh = lax.rem(zh0 + 1 + m // 4, 2)
        return 2 * x + zh

    def d_copy(m):
        return pltpu.make_async_remote_copy(
            src_ref=d_out.at[m], dst_ref=d_in.at[m],
            send_sem=d_ss.at[m], recv_sem=d_rs.at[m],
            device_id=(d_target(m), ti), device_id_type=MESH,
        )

    def docs_of(m, half, acc):
        rows = pl.ds(pl.multiple_of(d_target(m) * BLK, BLK), BLK)
        for slot in range(8 * half, 8 * half + 8):
            blk = static_block(slot)
            p = jnp.exp2(s_ref[slot, rows, :] - lse_ref[slot : slot + 1, :])
            u = (w_ref[slot : slot + 1, :] * p).astype(BF16)
            acc = acc + jnp.dot(u, q_ref[blk * BLK : (blk + 1) * BLK, :], preferred_element_type=F32)
        return acc

    def early(i, _):
        for m in (2 * i, 2 * i + 1):
            d_part[m] = docs_of(m, 0, jnp.zeros((BLK, DIM), F32))
        return 0

    global_lse(0)
    lax.fori_loop(0, 4, early, 0)
    finish(7, 1)
    send(7)
    global_lse(1)

    def late(m, _):
        d_out[m] = docs_of(m, 1, d_part[m]).astype(BF16)
        d_copy(m).start()
        return 0

    lax.fori_loop(0, 7, late, 0)
    d_part[7] = docs_of(7, 1, d_part[7])

    own_half = lax.rem(y0 + z0, 2)
    row = pl.ds(2 * y0 + core, 1)
    lse = lse_ref[pl.ds(8 * own_half + 2 * y0 + core, 1), :]

    def share(ys, zs):
        both = jnp.zeros((1, BLK), F32)
        for cs in range(2):
            k = lax.rem(ti - (4 * ys + 2 * zs + cs) + 16, 16)
            both = both + jnp.exp2(lse_all[own_half, k - 1, row, :] - lse)
        return both

    partner = jnp.where(core == 1, 0, 14)
    own_share = jnp.exp2(lse_mine[own_half, row, :] - lse) + jnp.exp2(lse_all[own_half, partner, row, :] - lse)
    own_step = jnp.where(own_half == 0, 3, 7)
    part[0] = part[own_step] * own_share
    for k in range(4):
        for z in range(2):
            slot = 2 * k + z

            def add(k=k, z=z, slot=slot):
                pltpu.make_async_remote_copy(
                    src_ref=q_out.at[0], dst_ref=q_in.at[slot],
                    send_sem=q_ss.at[0], recv_sem=q_rs.at[slot],
                    device_id=(qi, lax.rem(ti + 2, 16)), device_id_type=MESH,
                ).wait_recv()
                part[0] += q_in[slot].astype(F32) * share(lax.rem(y0 + 3 - k, 4), z)

            if k < 3:
                add()
            else:
                pl.when(z != z0)(add)
    gq_ref[...] = (part[0] * w_ref[pl.ds(8 * own_half + 2 * y0 + core, 1), :]).T
    total = d_part[7]
    for m in range(7):
        d_copy(m).wait_recv()
        total = total + d_in[m].astype(F32)
    gd_ref[0] = total

    for half in range(2):
        for k in range(1, 16):
            lse_copy(half, k).wait_send()
    for st in range(8):
        pair_copy(st).wait_send()

        @pl.when(is_remote(st))
        def _():
            q_copy(st).wait_send()

    for m in range(7):
        d_copy(m).wait_send()


def shards(queries, documents, cotangent):
    vmem = pl.BlockSpec(memory_space=pltpu.VMEM)
    dma = pltpu.SemaphoreType.DMA
    n_docs = documents.shape[0]
    return pl.pallas_call(
        kernel,
        out_shape=(
            jax.ShapeDtypeStruct((BLK, DIM), F32),
            jax.ShapeDtypeStruct((1, BLK, DIM), F32),
        ),
        in_specs=[vmem, vmem, pl.BlockSpec(memory_space=pltpu.SMEM)],
        out_specs=(vmem, vmem),
        scratch_shapes=[
            pltpu.VMEM((NBLK, n_docs, BLK), F32),
            pltpu.VMEM((n_docs, 2 * DIM), BF16),
            pltpu.VMEM((DIM, n_docs), BF16),
            pltpu.VMEM((NBLK, BLK), F32),
            pltpu.VMEM((2, 8, BLK), F32),
            pltpu.VMEM((2, 15, 8, BLK), F32),
            pltpu.VMEM((NBLK, BLK), F32),
            pltpu.VMEM((8, DIM + 8, BLK), F32),
            pltpu.VMEM((8, DIM + 8, BLK), F32),
            pltpu.VMEM((8, DIM, BLK), F32),
            pltpu.VMEM((8, DIM, BLK), BF16),
            pltpu.VMEM((8, DIM, BLK), BF16),
            pltpu.VMEM((8, BLK, DIM), F32),
            pltpu.VMEM((7, BLK, DIM), BF16),
            pltpu.VMEM((7, BLK, DIM), BF16),
            dma((2, 15)), dma((2, 15)), dma((8,)), dma((8,)),
            dma((8,)), dma((8,)), dma((7,)), dma((7,)),
        ],
        compiler_params=pltpu.CompilerParams(
            collective_id=0, has_side_effects=True, vmem_limit_bytes=67043328
        ),
    )(queries, documents, cotangent)


def solution(mesh):
    placed = (P("query", None), P("tok", None), P("query"))
    return jax.shard_map(
        shards,
        mesh=mesh,
        in_specs=placed,
        out_specs=(P(("query", "tok"), None), P("tok", "query", None)),
        check_vma=False,
    )
```

time: 40.8 us -> 47.4 us (1.16)
  the two profiles are of different devices: /device:TPU:1 before, /device:TPU:24 now
where the time goes in v3:
time: 47.4 us; the launch traced here: 47.3 us
  Pallas kernels  44.4 us (94%)
  local copies, waits for them, and re-layouts  2.26 us (5%)
  between operations  0.65 us (1%)
    pallas_call x1, Pallas kernels, shards(): pl.pallas_call(kernel, out_shape=(jax.ShapeDtypeStruct((BLK, DIM), F32),...  44.4 us
    unnamed x4, local copies, waits for them, and re-layouts  2.26 us

profile of v3, /device:TPU:24, one launch (start us, length us, event | category | flops | bytes accessed | tf_op | source)
XLA Modules:
  0.0 47.3 jit_solution(5686876991314014962)
XLA Ops:
  0.6 44.4 %shard_map.50 = (f32[256,128]{1,0:T(8,128)}, f32[1,256,128]{2,1,0:T(8,128)}) custom-call(bf16[4096,128]{1,0:T(8,128)(2,1)} %q_ref.1, bf16[2048,128]{1,0:T(8,128)(2,1)} %d_ref.1, f32[128]{0:T(128)} %cot_ref.1), custom_call_target="tpu_custom_call" | custom-call | tf_op jit(solution)/shard_map/pallas_call | solution.py:309
  45.0 0.0 copy-start
  45.0 1.6 %copy.7 = f32[256,128]{1,0:T(8,128)} copy(f32[256,128]{1,0:T(8,128)} %get-tuple-element.4) | data formatting | bytes 262144
  46.6 0.0 copy-done
  46.6 0.7 %copy.8 = f32[1,256,128]{2,1,0:T(8,128)} copy(f32[1,256,128]{2,1,0:T(8,128)S(1)} %copy-done) | data formatting | bytes 262144
Async XLA Ops:
  45.0 1.6 %copy-start = (f32[1,256,128]{2,1,0:T(8,128)S(1)}, f32[1,256,128]{2,1,0:T(8,128)}, u32[]{:S(2)}) copy-start(f32[1,256,128]{2,1,0:T(8,128)} %get-tuple-element.5) | copy-start | bytes 393220

commit v4 on v2

--- a/solution.py
+++ b/solution.py
@@ -23,6 +23,7 @@
 CHUNK = 256
 NCHUNK = 8
 SUBROWS = 16
+Z_COPY = None
 
 
 def block_of(slot):
@@ -33,7 +34,7 @@
 
 def kernel(
     q_ref, d_ref, cot_ref, gq_ref, gd_ref,
-    s_ref, u_ref, dc_ref, dt_ref, lse_mine, lse_all, lse_ref,
+    s_ref, u_ref, dc_ref, dt_ref, acc_ref, w_ref, lse_mine, lse_all, lse_ref,
     pair_out, pair_in, part, q_out, q_in, d_out, d_in, d_own,
     lse_ss, lse_rs, pair_ss, pair_rs, q_ss, q_rs, d_ss, d_rs,
 ):
@@ -44,8 +45,9 @@
     barrier = pltpu.get_barrier_semaphore()
     for k in range(1, 16):
         pl.semaphore_signal(barrier, inc=1, device_id=(qi, lax.rem(ti + k, 16)), device_id_type=MESH)
-    for k in range(1, 8):
-        pl.semaphore_signal(barrier, inc=1, device_id=(lax.rem(qi + k, 8), ti), device_id_type=MESH)
+    for k in range(1, 4):
+        pl.semaphore_signal(barrier, inc=1, device_id=(2 * lax.rem(x0 + k, 4) + zh0, ti), device_id_type=MESH)
+    pl.semaphore_signal(barrier, inc=1, device_id=(2 * x0 + 1 - zh0, ti), device_id_type=MESH)
 
     for c in range(NCHUNK):
         rows = slice(c * CHUNK, (c + 1) * CHUNK)
@@ -112,7 +114,7 @@
         )
 
     tops = lax.fori_loop(0, 4, step_a(0), (scores_of(0), scores_of(1)))
-    pl.semaphore_wait(barrier, 22)
+    pl.semaphore_wait(barrier, 19)
     for k in range(1, 16):
         lse_copy(0, k).start()
     tops = lax.fori_loop(4, 7, step_a(1), tops)
@@ -126,23 +128,30 @@
         lse_copy(1, k).start()
 
     lane_query = lax.broadcasted_iota(jnp.int32, (1, BLK), 1) // QLEN
-
-    def weights_of(block):
+    for slot in range(NBLK):
+        half, y, cb = slot // 8, (slot % 8) // 2, slot % 2
+        block = 4 * y + 2 * ((half + y) % 2) + cb
         w = jnp.zeros((1, BLK), F32)
         for g in range(BLK // QLEN):
             w = jnp.where(lane_query == g, cot_ref[block * (BLK // QLEN) + g], w)
-        return w
-
-    def probs_of(slot):
+        w_ref[slot : slot + 1, :] = w
+
+    def doc_rows(x, zh):
+        return pl.ds(pl.multiple_of((2 * x + zh) * BLK, BLK), BLK)
+
+    def probs_of(slot, zh, acc):
         lse = lse_ref[pl.ds(slot, 1), :]
-        w = weights_of(block_of(slot))
-        acc = jnp.zeros((DIM, BLK), F32)
-        for c in range(NCHUNK):
-            rows = slice(c * CHUNK, (c + 1) * CHUNK)
+        w = w_ref[pl.ds(slot, 1), :]
+        for x in range(4):
+            rows = doc_rows(x, zh)
             p = jnp.exp2(s_ref[slot, rows, :] - lse)
             u_ref[slot, rows, :] = (w * p).astype(BF16)
             acc = acc + jnp.dot(dt_ref[:, rows], p.astype(BF16), preferred_element_type=F32)
-        return (w * acc).T
+        return acc
+
+    def query_grads(slot):
+        acc = probs_of(slot, zh0, acc_ref[slot])
+        return (w_ref[pl.ds(slot, 1), :] * acc).T
 
     def pair_copy(st):
         return pltpu.make_async_remote_copy(
@@ -184,8 +193,8 @@
         for st in (2 * i, 2 * i + 1):
             _, y, _ = target(st)
             base = 8 * (st // 4) + 2 * y
-            pair_out[st] = probs_of(base + 1 - core)
-            part[st] = probs_of(base + core)
+            pair_out[st] = query_grads(base + 1 - core)
+            part[st] = query_grads(base + core)
         for st in (2 * i, 2 * i + 1):
             pair_copy(st).start()
 
@@ -208,21 +217,24 @@
         for k in range(15):
             total = total + jnp.exp2(lse_all[half, k] - top)
         lse_ref[8 * half : 8 * half + 8, :] = top + jnp.log2(total)
-        lax.fori_loop(2 * half, 2 * half + 2, step_b, 0)
+        for slot in range(8 * half, 8 * half + 8):
+            acc_ref[slot] = probs_of(slot, 1 - zh0, jnp.zeros((DIM, BLK), F32))
+
+    def d_target(m):
+        m = lax.rem(m, 4)
+        return lax.rem(x0 + jnp.where(m == 2, 3, jnp.where(m == 3, 0, 2 - m)), 4)
 
     def d_copy(m):
-        x = lax.rem(x0 + lax.rem(m, 4) + 1, 4)
-        zh = lax.rem(zh0 + 1 + m // 4, 2)
+        device = 2 * x0 + 1 - zh0 if m is Z_COPY else 2 * d_target(m) + zh0
+        m = 3 if m is Z_COPY else m
         return pltpu.make_async_remote_copy(
             src_ref=d_out.at[m], dst_ref=d_in.at[m],
             send_sem=d_ss.at[m], recv_sem=d_rs.at[m],
-            device_id=(2 * x + zh, ti), device_id_type=MESH,
+            device_id=(device, ti), device_id_type=MESH,
         )
 
-    def docs_of(m):
-        x = lax.rem(x0 + lax.rem(m, 4) + 1, 4)
-        zh = lax.rem(zh0 + 1 + m // 4, 2)
-        rows = pl.ds(pl.multiple_of((2 * x + zh) * BLK, BLK), BLK)
+    def docs_of(m, zh):
+        rows = doc_rows(d_target(m), zh)
         acc = jnp.zeros((BLK, DIM), F32)
         for slot in range(NBLK):
             half, y, cb = slot // 8, (slot % 8) // 2, slot % 2
@@ -232,18 +244,31 @@
             )
         return acc
 
-    def step_c(m, _):
-        d_out[m] = docs_of(m).astype(BF16)
-        d_copy(m).start()
-        return 0
-
-    lax.fori_loop(0, 1, step_c, 0)
+    def step_c(zh):
+        def body(m, _):
+            d_out[m] = docs_of(m, zh).astype(BF16)
+            d_copy(m).start()
+            return 0
+
+        return body
+
+    lax.fori_loop(0, 3, step_c(1 - zh0), 0)
+    d_own[...] = docs_of(3, 1 - zh0)
+    lax.fori_loop(0, 4, step_b, 0)
+    for m in range(3):
+        d_copy(m).wait_recv()
+    total = d_own[...]
+    for m in range(3):
+        total = total + d_in[m].astype(F32)
+    d_out[3] = total.astype(BF16)
+    lax.fori_loop(4, 5, step_c(zh0), 0)
+    d_copy(Z_COPY).start()
     for st in (6, 7):
         finish(st)
     for st in (6, 7):
         send(st)
-    lax.fori_loop(1, 7, step_c, 0)
-    d_own[...] = docs_of(7)
+    lax.fori_loop(5, 7, step_c(zh0), 0)
+    d_own[...] = docs_of(7, zh0)
 
     mine = jnp.where(lax.rem(y0 + z0, 2) == 0, 3, 7)
     gq_ref[...] = part[mine]
@@ -265,9 +290,9 @@
             else:
                 pl.when(z != z0)(add)
     total = d_own[...]
-    for m in range(7):
+    for m in (Z_COPY, 4, 5, 6):
         d_copy(m).wait_recv()
-        total = total + d_in[m].astype(F32)
+        total = total + d_in[3 if m is Z_COPY else m].astype(F32)
     gd_ref[0] = total
 
     for half in range(2):
@@ -280,7 +305,7 @@
         def _():
             q_copy(st).wait_send()
 
-    for m in range(7):
+    for m in (0, 1, 2, Z_COPY, 4, 5, 6):
         d_copy(m).wait_send()
 
 
@@ -301,6 +326,8 @@
             pltpu.VMEM((NBLK, n_docs, BLK), BF16),
             pltpu.VMEM((n_docs, 2 * DIM), BF16),
             pltpu.VMEM((DIM, n_docs), BF16),
+            pltpu.VMEM((NBLK, DIM, BLK), F32),
+            pltpu.VMEM((NBLK, BLK), F32),
             pltpu.VMEM((2, 8, BLK), F32),
             pltpu.VMEM((2, 15, 8, BLK), F32),
             pltpu.VMEM((NBLK, BLK), F32),

time: 40.8 us -> 40.9 us (level)
  no operation moved by 1% of the time
where the time goes in v4:
time: 40.9 us; the launch traced here: 40.6 us
  Pallas kernels  37.7 us (92%)
  local copies, waits for them, and re-layouts  2.26 us (6%)
  between operations  0.65 us (2%)
    pallas_call x1, Pallas kernels, shards(): pl.pallas_call(kernel, out_shape=(jax.ShapeDtypeStruct((BLK, DIM), F32),...  37.7 us
    unnamed x4, local copies, waits for them, and re-layouts  2.26 us

profile of v4, /device:TPU:1, one launch (start us, length us, event | category | flops | bytes accessed | tf_op | source)
XLA Modules:
  0.0 40.6 jit_solution(12259659074494112478)
XLA Ops:
  0.6 37.7 %shard_map.50 = (f32[256,128]{1,0:T(8,128)}, f32[1,256,128]{2,1,0:T(8,128)}) custom-call(bf16[4096,128]{1,0:T(8,128)(2,1)} %q_ref.1, bf16[2048,128]{1,0:T(8,128)(2,1)} %d_ref.1, f32[128]{0:T(128)} %cot_ref.1), custom_call_target="tpu_custom_call" | custom-call | tf_op jit(solution)/shard_map/pallas_call | solution.py:316
  38.3 0.0 copy-start
  38.3 1.6 %copy.7 = f32[256,128]{1,0:T(8,128)} copy(f32[256,128]{1,0:T(8,128)} %get-tuple-element.4) | data formatting | bytes 262144
  39.9 0.0 copy-done
  39.9 0.7 %copy.8 = f32[1,256,128]{2,1,0:T(8,128)} copy(f32[1,256,128]{2,1,0:T(8,128)S(1)} %copy-done) | data formatting | bytes 262144
Async XLA Ops:
  38.3 1.6 %copy-start = (f32[1,256,128]{2,1,0:T(8,128)S(1)}, f32[1,256,128]{2,1,0:T(8,128)}, u32[]{:S(2)}) copy-start(f32[1,256,128]{2,1,0:T(8,128)} %get-tuple-element.5) | copy-start | bytes 393220

commit v5 on v4

--- a/solution.py
+++ b/solution.py
@@ -24,6 +24,7 @@
 NCHUNK = 8
 SUBROWS = 16
 Z_COPY = None
+VMEM_LIMIT = 62 * 2**20
 
 
 def block_of(slot):
@@ -34,7 +35,7 @@
 
 def kernel(
     q_ref, d_ref, cot_ref, gq_ref, gd_ref,
-    s_ref, u_ref, dc_ref, dt_ref, acc_ref, w_ref, lse_mine, lse_all, lse_ref,
+    s_ref, u_ref, dc_ref, dt_ref, w_ref, lse_mine, lse_all, lse_ref,
     pair_out, pair_in, part, q_out, q_in, d_out, d_in, d_own,
     lse_ss, lse_rs, pair_ss, pair_rs, q_ss, q_rs, d_ss, d_rs,
 ):
@@ -139,19 +140,16 @@
     def doc_rows(x, zh):
         return pl.ds(pl.multiple_of((2 * x + zh) * BLK, BLK), BLK)
 
-    def probs_of(slot, zh, acc):
+    def query_grads(slot):
         lse = lse_ref[pl.ds(slot, 1), :]
         w = w_ref[pl.ds(slot, 1), :]
-        for x in range(4):
-            rows = doc_rows(x, zh)
+        acc = jnp.zeros((DIM, BLK), F32)
+        for c in range(NCHUNK):
+            rows = slice(c * CHUNK, (c + 1) * CHUNK)
             p = jnp.exp2(s_ref[slot, rows, :] - lse)
             u_ref[slot, rows, :] = (w * p).astype(BF16)
             acc = acc + jnp.dot(dt_ref[:, rows], p.astype(BF16), preferred_element_type=F32)
-        return acc
-
-    def query_grads(slot):
-        acc = probs_of(slot, zh0, acc_ref[slot])
-        return (w_ref[pl.ds(slot, 1), :] * acc).T
+        return (w * acc).T
 
     def pair_copy(st):
         return pltpu.make_async_remote_copy(
@@ -217,8 +215,7 @@
         for k in range(15):
             total = total + jnp.exp2(lse_all[half, k] - top)
         lse_ref[8 * half : 8 * half + 8, :] = top + jnp.log2(total)
-        for slot in range(8 * half, 8 * half + 8):
-            acc_ref[slot] = probs_of(slot, 1 - zh0, jnp.zeros((DIM, BLK), F32))
+        lax.fori_loop(2 * half, 2 * half + 2, step_b, 0)
 
     def d_target(m):
         m = lax.rem(m, 4)
@@ -252,22 +249,20 @@
 
         return body
 
-    lax.fori_loop(0, 3, step_c(1 - zh0), 0)
-    d_own[...] = docs_of(3, 1 - zh0)
-    lax.fori_loop(0, 4, step_b, 0)
-    for m in range(3):
-        d_copy(m).wait_recv()
-    total = d_own[...]
-    for m in range(3):
-        total = total + d_in[m].astype(F32)
-    d_out[3] = total.astype(BF16)
-    lax.fori_loop(4, 5, step_c(zh0), 0)
-    d_copy(Z_COPY).start()
+    lax.fori_loop(0, 1, step_c(1 - zh0), 0)
     for st in (6, 7):
         finish(st)
     for st in (6, 7):
         send(st)
-    lax.fori_loop(5, 7, step_c(zh0), 0)
+    lax.fori_loop(1, 3, step_c(1 - zh0), 0)
+    d_own[...] = docs_of(3, 1 - zh0)
+    lax.fori_loop(4, 7, step_c(zh0), 0)
+    total = d_own[...]
+    for m in range(3):
+        d_copy(m).wait_recv()
+        total = total + d_in[m].astype(F32)
+    d_out[3] = total.astype(BF16)
+    d_copy(Z_COPY).start()
     d_own[...] = docs_of(7, zh0)
 
     mine = jnp.where(lax.rem(y0 + z0, 2) == 0, 3, 7)
@@ -309,15 +304,23 @@
         d_copy(m).wait_send()
 
 
+def put_out(gq_in, gd_in, gq_out, gd_out, sems):
+    copies = [pltpu.make_async_copy(gq_in, gq_out, sems.at[0]), pltpu.make_async_copy(gd_in, gd_out, sems.at[1])]
+    for copy in copies:
+        copy.start()
+    for copy in copies:
+        copy.wait()
+
+
 def shards(queries, documents, cotangent):
     vmem = pl.BlockSpec(memory_space=pltpu.VMEM)
     dma = pltpu.SemaphoreType.DMA
     n_docs = documents.shape[0]
-    return pl.pallas_call(
+    grads = pl.pallas_call(
         kernel,
         out_shape=(
-            jax.ShapeDtypeStruct((BLK, DIM), F32),
-            jax.ShapeDtypeStruct((1, BLK, DIM), F32),
+            pltpu.VMEM((BLK, DIM), F32),
+            pltpu.VMEM((1, BLK, DIM), F32),
         ),
         in_specs=[vmem, vmem, pl.BlockSpec(memory_space=pltpu.SMEM)],
         out_specs=(vmem, vmem),
@@ -326,7 +329,6 @@
             pltpu.VMEM((NBLK, n_docs, BLK), BF16),
             pltpu.VMEM((n_docs, 2 * DIM), BF16),
             pltpu.VMEM((DIM, n_docs), BF16),
-            pltpu.VMEM((NBLK, DIM, BLK), F32),
             pltpu.VMEM((NBLK, BLK), F32),
             pltpu.VMEM((2, 8, BLK), F32),
             pltpu.VMEM((2, 15, 8, BLK), F32),
@@ -343,9 +345,20 @@
             dma((8,)), dma((8,)), dma((7,)), dma((7,)),
         ],
         compiler_params=pltpu.CompilerParams(
-            collective_id=0, has_side_effects=True, vmem_limit_bytes=67043328
+            collective_id=0, has_side_effects=True, vmem_limit_bytes=VMEM_LIMIT
         ),
     )(queries, documents, cotangent)
+    anywhere = pl.BlockSpec(memory_space=pl.ANY)
+    return pl.pallas_call(
+        put_out,
+        out_shape=(
+            jax.ShapeDtypeStruct((BLK, DIM), F32),
+            jax.ShapeDtypeStruct((1, BLK, DIM), F32),
+        ),
+        in_specs=[vmem, vmem],
+        out_specs=(anywhere, anywhere),
+        scratch_shapes=[dma((2,))],
+    )(*(pltpu.with_memory_space_constraint(g, pltpu.VMEM) for g in grads))
 
 
 def solution(mesh):

time: 40.9 us -> 35.4 us (0.87)
  Pallas kernels: 37.7 us -> 34.7 us
  local copies, waits for them, and re-layouts: 2.26 us -> 0 us
    pallas_call x1 -> x2, Pallas kernels: 37.7 us -> 34.7 us  [the longest x1 33.9 us: shards(): pl.pallas_call(kernel, out_shape=(pltpu.VMEM((BLK, DIM), F32), pltpu.VMEM...]
    unnamed x4 -> x0, local copies, waits for them, and re-layouts: 2.26 us -> none
where the time goes in v5:
time: 35.4 us; the launch traced here: 35.3 us
  Pallas kernels  34.7 us (98%)
  between operations  0.64 us (2%)
    pallas_call x1, Pallas kernels, shards(): pl.pallas_call(kernel, out_shape=(pltpu.VMEM((BLK, DIM), F32), pltpu.VMEM...  33.9 us
    pallas_call x1, Pallas kernels, shards(): pl.pallas_call(put_out, out_shape=(jax.ShapeDtypeStruct((BLK, DIM), F32),...  0.72 us

profile of v5, /device:TPU:1, one launch (start us, length us, event | category | flops | bytes accessed | tf_op | source)
XLA Modules:
  0.0 35.3 jit_solution(11749474078416889589)
XLA Ops:
  0.6 33.9 %shard_map.50 = (f32[256,128]{1,0:T(8,128)S(1)}, f32[1,256,128]{2,1,0:T(8,128)S(1)}) custom-call(bf16[4096,128]{1,0:T(8,128)(2,1)} %q_ref.1, bf16[2048,128]{1,0:T(8,128)(2,1)} %d_ref.1, f32[128]{0:T(128)} %cot_ref.1), custom_call_target="tpu_custom_call" | custom-call | tf_op jit(solution)/shard_map/pallas_call | solution.py:319
  34.6 0.7 %shard_map.51 = (f32[256,128]{1,0:T(8,128)}, f32[1,256,128]{2,1,0:T(8,128)}) custom-call(f32[256,128]{1,0:T(8,128)S(1)} %get-tuple-element.4.gq_in, f32[1,256,128]{2,1,0:T(8,128)S(1)} %get-tuple-element.5.gd_in), custom_call_target="tpu_custom_call" | custom-call | tf_op jit(solution)/shard_map/pallas_call | solution.py:352

commit v6 on v5

--- a/solution.py
+++ b/solution.py
@@ -24,6 +24,7 @@
 NCHUNK = 8
 SUBROWS = 16
 Z_COPY = None
+GROUPS = ((0, slice(0, 8)), (1, slice(0, 4)), (1, slice(4, 8)))
 VMEM_LIMIT = 62 * 2**20
 
 
@@ -34,7 +35,8 @@
 
 
 def kernel(
-    q_ref, d_ref, cot_ref, gq_ref, gd_ref,
+    q_in_hbm, d_in_hbm, cot_ref, gq_ref, gd_ref,
+    q_ref, d_ref, in_sems,
     s_ref, u_ref, dc_ref, dt_ref, w_ref, lse_mine, lse_all, lse_ref,
     pair_out, pair_in, part, q_out, q_in, d_out, d_in, d_own,
     lse_ss, lse_rs, pair_ss, pair_rs, q_ss, q_rs, d_ss, d_rs,
@@ -43,6 +45,10 @@
     x0, zh0 = qi // 2, lax.rem(qi, 2)
     y0, z0, core = ti // 4, lax.rem(ti // 2, 2), lax.rem(ti, 2)
 
+    fetch_d = pltpu.make_async_copy(d_in_hbm, d_ref, in_sems.at[0])
+    fetch_q = pltpu.make_async_copy(q_in_hbm, q_ref, in_sems.at[1])
+    fetch_d.start()
+    fetch_q.start()
     barrier = pltpu.get_barrier_semaphore()
     for k in range(1, 16):
         pl.semaphore_signal(barrier, inc=1, device_id=(qi, lax.rem(ti + k, 16)), device_id_type=MESH)
@@ -50,12 +56,15 @@
         pl.semaphore_signal(barrier, inc=1, device_id=(2 * lax.rem(x0 + k, 4) + zh0, ti), device_id_type=MESH)
     pl.semaphore_signal(barrier, inc=1, device_id=(2 * x0 + 1 - zh0, ti), device_id_type=MESH)
 
+    fetch_d.wait()
     for c in range(NCHUNK):
         rows = slice(c * CHUNK, (c + 1) * CHUNK)
         scaled = d_ref[rows, :].astype(F32) * SCALE
         high = scaled.astype(BF16)
         dc_ref[rows, 0:DIM] = high
         dc_ref[rows, DIM : 2 * DIM] = (scaled - high.astype(F32)).astype(BF16)
+
+    fetch_q.wait()
 
     def q_pair(slot):
         rows = q_ref[pl.ds(pl.multiple_of(block_of(slot) * BLK, BLK), BLK), :]
@@ -107,10 +116,11 @@
 
         return body
 
-    def lse_copy(half, k):
+    def lse_copy(group, k):
+        half, rows = GROUPS[group]
         return pltpu.make_async_remote_copy(
-            src_ref=lse_mine.at[half], dst_ref=lse_all.at[half, k - 1],
-            send_sem=lse_ss.at[half, k - 1], recv_sem=lse_rs.at[half, k - 1],
+            src_ref=lse_mine.at[half, rows], dst_ref=lse_all.at[half, k - 1, rows],
+            send_sem=lse_ss.at[group, k - 1], recv_sem=lse_rs.at[group, k - 1],
             device_id=(qi, lax.rem(ti + k, 16)), device_id_type=MESH,
         )
 
@@ -118,7 +128,10 @@
     pl.semaphore_wait(barrier, 19)
     for k in range(1, 16):
         lse_copy(0, k).start()
-    tops = lax.fori_loop(4, 7, step_a(1), tops)
+    tops = lax.fori_loop(4, 6, step_a(1), tops)
+    for k in range(1, 16):
+        lse_copy(1, k).start()
+    tops = lax.fori_loop(6, 7, step_a(1), tops)
     turn(7)
     for k in range(2):
         total = None
@@ -126,7 +139,7 @@
             total = exp_chunk(14 + k, c, tops[k], total)
         local_lse(1, 6 + k, tops[k], total)
     for k in range(1, 16):
-        lse_copy(1, k).start()
+        lse_copy(2, k).start()
 
     lane_query = lax.broadcasted_iota(jnp.int32, (1, BLK), 1) // QLEN
     for slot in range(NBLK):
@@ -160,12 +173,12 @@
 
     def target(st):
         half, k = st // 4, lax.rem(st, 4)
-        y = lax.rem(y0 + 1 + k, 4)
-        return k, y, lax.rem(half + y, 2)
+        y = 2 * (k // 2) + lax.rem(y0 + 1 + k, 2)
+        return y, lax.rem(half + y, 2)
 
     def q_copy(st):
-        k, y, z = target(st)
-        slot = 2 * k + z0
+        y, z = target(st)
+        slot = 2 * y0 + z0
         return pltpu.make_async_remote_copy(
             src_ref=q_out.at[st], dst_ref=q_in.at[slot],
             send_sem=q_ss.at[st], recv_sem=q_rs.at[slot],
@@ -179,8 +192,8 @@
         q_out[st] = both.astype(BF16)
 
     def is_remote(st):
-        k, y, z = target(st)
-        return jnp.logical_or(k != 3, z != z0)
+        y, z = target(st)
+        return 2 * y + z != 2 * y0 + z0
 
     def send(st):
         @pl.when(is_remote(st))
@@ -189,7 +202,7 @@
 
     def step_b(i, _):
         for st in (2 * i, 2 * i + 1):
-            _, y, _ = target(st)
+            y, _ = target(st)
             base = 8 * (st // 4) + 2 * y
             pair_out[st] = query_grads(base + 1 - core)
             part[st] = query_grads(base + core)
@@ -205,17 +218,17 @@
 
         return 0
 
-    for half in range(2):
+    for group, (half, rows) in enumerate(GROUPS):
         for k in range(1, 16):
-            lse_copy(half, k).wait_recv()
-        top = lse_mine[half]
+            lse_copy(group, k).wait_recv()
+        top = lse_mine[half, rows]
         for k in range(15):
-            top = jnp.maximum(top, lse_all[half, k])
-        total = jnp.exp2(lse_mine[half] - top)
+            top = jnp.maximum(top, lse_all[half, k, rows])
+        total = jnp.exp2(lse_mine[half, rows] - top)
         for k in range(15):
-            total = total + jnp.exp2(lse_all[half, k] - top)
-        lse_ref[8 * half : 8 * half + 8, :] = top + jnp.log2(total)
-        lax.fori_loop(2 * half, 2 * half + 2, step_b, 0)
+            total = total + jnp.exp2(lse_all[half, k, rows] - top)
+        lse_ref[8 * half + rows.start : 8 * half + rows.stop, :] = top + jnp.log2(total)
+        lax.fori_loop(group + 1 if group else 0, group + 2, step_b, 0)
 
     def d_target(m):
         m = lax.rem(m, 4)
@@ -265,34 +278,27 @@
     d_copy(Z_COPY).start()
     d_own[...] = docs_of(7, zh0)
 
-    mine = jnp.where(lax.rem(y0 + z0, 2) == 0, 3, 7)
-    gq_ref[...] = part[mine]
-    for k in range(4):
-        for z in range(2):
-            slot = 2 * k + z
-
-            def add(slot=slot):
-                q_copy_in = pltpu.make_async_remote_copy(
-                    src_ref=q_out.at[0], dst_ref=q_in.at[slot],
-                    send_sem=q_ss.at[0], recv_sem=q_rs.at[slot],
-                    device_id=(qi, lax.rem(ti + 2, 16)), device_id_type=MESH,
-                )
-                q_copy_in.wait_recv()
-                gq_ref[...] += q_in[slot].astype(F32)
-
-            if k < 3:
-                add()
-            else:
-                pl.when(z != z0)(add)
+    gq_ref[...] = part[4 * lax.rem(y0 + z0, 2) + 2 * (y0 // 2) + 1]
+    for slot in range(8):
+
+        @pl.when(slot != 2 * y0 + z0)
+        def _():
+            pltpu.make_async_remote_copy(
+                src_ref=q_out.at[0], dst_ref=q_in.at[slot],
+                send_sem=q_ss.at[0], recv_sem=q_rs.at[slot],
+                device_id=(qi, lax.rem(ti + 2, 16)), device_id_type=MESH,
+            ).wait_recv()
+            gq_ref[...] += q_in[slot].astype(F32)
+
     total = d_own[...]
     for m in (Z_COPY, 4, 5, 6):
         d_copy(m).wait_recv()
         total = total + d_in[3 if m is Z_COPY else m].astype(F32)
     gd_ref[0] = total
 
-    for half in range(2):
+    for group in range(3):
         for k in range(1, 16):
-            lse_copy(half, k).wait_send()
+            lse_copy(group, k).wait_send()
     for st in range(8):
         pair_copy(st).wait_send()
 
@@ -314,6 +320,7 @@
 
 def shards(queries, documents, cotangent):
     vmem = pl.BlockSpec(memory_space=pltpu.VMEM)
+    anywhere = pl.BlockSpec(memory_space=pl.ANY)
     dma = pltpu.SemaphoreType.DMA
     n_docs = documents.shape[0]
     grads = pl.pallas_call(
@@ -322,9 +329,12 @@
             pltpu.VMEM((BLK, DIM), F32),
             pltpu.VMEM((1, BLK, DIM), F32),
         ),
-        in_specs=[vmem, vmem, pl.BlockSpec(memory_space=pltpu.SMEM)],
+        in_specs=[anywhere, anywhere, pl.BlockSpec(memory_space=pltpu.SMEM)],
         out_specs=(vmem, vmem),
         scratch_shapes=[
+            pltpu.VMEM(queries.shape, BF16),
+            pltpu.VMEM(documents.shape, BF16),
+            dma((2,)),
             pltpu.VMEM((NBLK, n_docs, BLK), F32),
             pltpu.VMEM((NBLK, n_docs, BLK), BF16),
             pltpu.VMEM((n_docs, 2 * DIM), BF16),
@@ -341,14 +351,13 @@
             pltpu.VMEM((7, BLK, DIM), BF16),
             pltpu.VMEM((7, BLK, DIM), BF16),
             pltpu.VMEM((BLK, DIM), F32),
-            dma((2, 15)), dma((2, 15)), dma((8,)), dma((8,)),
+            dma((3, 15)), dma((3, 15)), dma((8,)), dma((8,)),
             dma((8,)), dma((8,)), dma((7,)), dma((7,)),
         ],
         compiler_params=pltpu.CompilerParams(
             collective_id=0, has_side_effects=True, vmem_limit_bytes=VMEM_LIMIT
         ),
     )(queries, documents, cotangent)
-    anywhere = pl.BlockSpec(memory_space=pl.ANY)
     return pl.pallas_call(
         put_out,
         out_shape=(

time: 35.4 us -> 36.2 us (1.023)
  Pallas kernels: 34.7 us -> 35.4 us
    pallas_call x1, Pallas kernels: 33.9 us -> 34.7 us  [shards(): pl.pallas_call(kernel, out_shape=(pltpu.VMEM((BLK, DIM), F32), pltpu.VMEM...]
where the time goes in v6:
time: 36.2 us; the launch traced here: 36 us
  Pallas kernels  35.4 us (98%)
  between operations  0.64 us (2%)
    pallas_call x1, Pallas kernels, shards(): pl.pallas_call(kernel, out_shape=(pltpu.VMEM((BLK, DIM), F32), pltpu.VMEM...  34.7 us

profile of v6, /device:TPU:1, one launch (start us, length us, event | category | flops | bytes accessed | tf_op | source)
XLA Modules:
  0.0 36.0 jit_solution(13395819281943702953)
XLA Ops:
  0.6 34.7 %shard_map.50 = (f32[256,128]{1,0:T(8,128)S(1)}, f32[1,256,128]{2,1,0:T(8,128)S(1)}) custom-call(bf16[4096,128]{1,0:T(8,128)(2,1)} %q_in_hbm.1, bf16[2048,128]{1,0:T(8,128)(2,1)} %d_in_hbm.1, f32[128]{0:T(128)} %cot_ref.1), custom_call_target="tpu_custom_call" | custom-call | tf_op jit(solution)/shard_map/pallas_call | solution.py:326
  35.3 0.7 %shard_map.51 = (f32[256,128]{1,0:T(8,128)}, f32[1,256,128]{2,1,0:T(8,128)}) custom-call(f32[256,128]{1,0:T(8,128)S(1)} %get-tuple-element.4.gq_in, f32[1,256,128]{2,1,0:T(8,128)S(1)} %get-tuple-element.5.gd_in), custom_call_target="tpu_custom_call" | custom-call | tf_op jit(solution)/shard_map/pallas_call | solution.py:361

commit v7 on v5

--- a/solution.py
+++ b/solution.py
@@ -34,7 +34,8 @@
 
 
 def kernel(
-    q_ref, d_ref, cot_ref, gq_ref, gd_ref,
+    q_in_hbm, d_in_hbm, cot_ref, gq_ref, gd_ref,
+    q_ref, d_ref, in_sems,
     s_ref, u_ref, dc_ref, dt_ref, w_ref, lse_mine, lse_all, lse_ref,
     pair_out, pair_in, part, q_out, q_in, d_out, d_in, d_own,
     lse_ss, lse_rs, pair_ss, pair_rs, q_ss, q_rs, d_ss, d_rs,
@@ -43,6 +44,10 @@
     x0, zh0 = qi // 2, lax.rem(qi, 2)
     y0, z0, core = ti // 4, lax.rem(ti // 2, 2), lax.rem(ti, 2)
 
+    fetch_d = pltpu.make_async_copy(d_in_hbm, d_ref, in_sems.at[0])
+    fetch_q = pltpu.make_async_copy(q_in_hbm, q_ref, in_sems.at[1])
+    fetch_d.start()
+    fetch_q.start()
     barrier = pltpu.get_barrier_semaphore()
     for k in range(1, 16):
         pl.semaphore_signal(barrier, inc=1, device_id=(qi, lax.rem(ti + k, 16)), device_id_type=MESH)
@@ -50,12 +55,15 @@
         pl.semaphore_signal(barrier, inc=1, device_id=(2 * lax.rem(x0 + k, 4) + zh0, ti), device_id_type=MESH)
     pl.semaphore_signal(barrier, inc=1, device_id=(2 * x0 + 1 - zh0, ti), device_id_type=MESH)
 
+    fetch_d.wait()
     for c in range(NCHUNK):
         rows = slice(c * CHUNK, (c + 1) * CHUNK)
         scaled = d_ref[rows, :].astype(F32) * SCALE
         high = scaled.astype(BF16)
         dc_ref[rows, 0:DIM] = high
         dc_ref[rows, DIM : 2 * DIM] = (scaled - high.astype(F32)).astype(BF16)
+
+    fetch_q.wait()
 
     def q_pair(slot):
         rows = q_ref[pl.ds(pl.multiple_of(block_of(slot) * BLK, BLK), BLK), :]
@@ -314,6 +322,7 @@
 
 def shards(queries, documents, cotangent):
     vmem = pl.BlockSpec(memory_space=pltpu.VMEM)
+    anywhere = pl.BlockSpec(memory_space=pl.ANY)
     dma = pltpu.SemaphoreType.DMA
     n_docs = documents.shape[0]
     grads = pl.pallas_call(
@@ -322,9 +331,12 @@
             pltpu.VMEM((BLK, DIM), F32),
             pltpu.VMEM((1, BLK, DIM), F32),
         ),
-        in_specs=[vmem, vmem, pl.BlockSpec(memory_space=pltpu.SMEM)],
+        in_specs=[anywhere, anywhere, pl.BlockSpec(memory_space=pltpu.SMEM)],
         out_specs=(vmem, vmem),
         scratch_shapes=[
+            pltpu.VMEM(queries.shape, BF16),
+            pltpu.VMEM(documents.shape, BF16),
+            dma((2,)),
             pltpu.VMEM((NBLK, n_docs, BLK), F32),
             pltpu.VMEM((NBLK, n_docs, BLK), BF16),
             pltpu.VMEM((n_docs, 2 * DIM), BF16),
@@ -348,7 +360,6 @@
             collective_id=0, has_side_effects=True, vmem_limit_bytes=VMEM_LIMIT
         ),
     )(queries, documents, cotangent)
-    anywhere = pl.BlockSpec(memory_space=pl.ANY)
     return pl.pallas_call(
         put_out,
         out_shape=(

time: 35.4 us -> 35.9 us (1.014)
  Pallas kernels: 34.7 us -> 35.1 us
    pallas_call x1, Pallas kernels: 33.9 us -> 34.4 us  [shards(): pl.pallas_call(kernel, out_shape=(pltpu.VMEM((BLK, DIM), F32), pltpu.VMEM...]
where the time goes in v7:
time: 35.9 us; the launch traced here: 35.8 us
  Pallas kernels  35.1 us (98%)
  between operations  0.64 us (2%)
    pallas_call x1, Pallas kernels, shards(): pl.pallas_call(kernel, out_shape=(pltpu.VMEM((BLK, DIM), F32), pltpu.VMEM...  34.4 us

profile of v7, /device:TPU:1, one launch (start us, length us, event | category | flops | bytes accessed | tf_op | source)
XLA Modules:
  0.0 35.8 jit_solution(15732765000434270509)
XLA Ops:
  0.6 34.4 %shard_map.50 = (f32[256,128]{1,0:T(8,128)S(1)}, f32[1,256,128]{2,1,0:T(8,128)S(1)}) custom-call(bf16[4096,128]{1,0:T(8,128)(2,1)} %q_in_hbm.1, bf16[2048,128]{1,0:T(8,128)(2,1)} %d_in_hbm.1, f32[128]{0:T(128)} %cot_ref.1), custom_call_target="tpu_custom_call" | custom-call | tf_op jit(solution)/shard_map/pallas_call | solution.py:328
  35.0 0.7 %shard_map.51 = (f32[256,128]{1,0:T(8,128)}, f32[1,256,128]{2,1,0:T(8,128)}) custom-call(f32[256,128]{1,0:T(8,128)S(1)} %get-tuple-element.4.gq_in, f32[1,256,128]{2,1,0:T(8,128)S(1)} %get-tuple-element.5.gd_in), custom_call_target="tpu_custom_call" | custom-call | tf_op jit(solution)/shard_map/pallas_call | solution.py:363

commit v8 on v5

--- a/solution.py
+++ b/solution.py
@@ -36,7 +36,7 @@
 def kernel(
     q_ref, d_ref, cot_ref, gq_ref, gd_ref,
     s_ref, u_ref, dc_ref, dt_ref, w_ref, lse_mine, lse_all, lse_ref,
-    pair_out, pair_in, part, q_out, q_in, d_out, d_in, d_own,
+    pair_out, pair_in, part, q_out, q_in, d_part, d_out, d_in, d_own,
     lse_ss, lse_rs, pair_ss, pair_rs, q_ss, q_rs, d_ss, d_rs,
 ):
     qi, ti = lax.axis_index("query"), lax.axis_index("tok")
@@ -187,6 +187,24 @@
         def _():
             q_copy(st).start()
 
+    def d_target(m):
+        m = lax.rem(m, 4)
+        return lax.rem(x0 + jnp.where(m == 2, 3, jnp.where(m == 3, 0, 2 - m)), 4)
+
+    def docs_of(m, zh, slots=range(NBLK), acc=None):
+        rows = doc_rows(d_target(m), zh)
+        for slot in slots:
+            half, y, cb = slot // 8, (slot % 8) // 2, slot % 2
+            blk = 4 * y + 2 * ((half + y) % 2) + cb
+            term = jnp.dot(u_ref[slot, rows, :], q_ref[blk * BLK : (blk + 1) * BLK, :], preferred_element_type=F32)
+            acc = term if acc is None else acc + term
+        return acc
+
+    def early_docs(i, _):
+        for m in (2 * i, 2 * i + 1):
+            d_part[m] = docs_of(m, 1 - zh0, range(8))
+        return 0
+
     def step_b(i, _):
         for st in (2 * i, 2 * i + 1):
             _, y, _ = target(st)
@@ -216,10 +234,8 @@
             total = total + jnp.exp2(lse_all[half, k] - top)
         lse_ref[8 * half : 8 * half + 8, :] = top + jnp.log2(total)
         lax.fori_loop(2 * half, 2 * half + 2, step_b, 0)
-
-    def d_target(m):
-        m = lax.rem(m, 4)
-        return lax.rem(x0 + jnp.where(m == 2, 3, jnp.where(m == 3, 0, 2 - m)), 4)
+        if half == 0:
+            lax.fori_loop(0, 2, early_docs, 0)
 
     def d_copy(m):
         device = 2 * x0 + 1 - zh0 if m is Z_COPY else 2 * d_target(m) + zh0
@@ -230,33 +246,23 @@
             device_id=(device, ti), device_id_type=MESH,
         )
 
-    def docs_of(m, zh):
-        rows = doc_rows(d_target(m), zh)
-        acc = jnp.zeros((BLK, DIM), F32)
-        for slot in range(NBLK):
-            half, y, cb = slot // 8, (slot % 8) // 2, slot % 2
-            blk = 4 * y + 2 * ((half + y) % 2) + cb
-            acc = acc + jnp.dot(
-                u_ref[slot, rows, :], q_ref[blk * BLK : (blk + 1) * BLK, :], preferred_element_type=F32
-            )
-        return acc
-
-    def step_c(zh):
-        def body(m, _):
-            d_out[m] = docs_of(m, zh).astype(BF16)
-            d_copy(m).start()
-            return 0
-
-        return body
-
-    lax.fori_loop(0, 1, step_c(1 - zh0), 0)
+    def step_cross(m, _):
+        d_out[m] = docs_of(m, 1 - zh0, range(8, NBLK), d_part[m]).astype(BF16)
+        d_copy(m).start()
+        return 0
+
+    def step_same(m, _):
+        d_out[m] = docs_of(m, zh0).astype(BF16)
+        d_copy(m).start()
+        return 0
+
+    lax.fori_loop(0, 3, step_cross, 0)
     for st in (6, 7):
         finish(st)
     for st in (6, 7):
         send(st)
-    lax.fori_loop(1, 3, step_c(1 - zh0), 0)
-    d_own[...] = docs_of(3, 1 - zh0)
-    lax.fori_loop(4, 7, step_c(zh0), 0)
+    d_own[...] = docs_of(3, 1 - zh0, range(8, NBLK), d_part[3])
+    lax.fori_loop(4, 7, step_same, 0)
     total = d_own[...]
     for m in range(3):
         d_copy(m).wait_recv()
@@ -338,6 +344,7 @@
             pltpu.VMEM((8, BLK, DIM), F32),
             pltpu.VMEM((8, BLK, DIM), BF16),
             pltpu.VMEM((8, BLK, DIM), BF16),
+            pltpu.VMEM((4, BLK, DIM), F32),
             pltpu.VMEM((7, BLK, DIM), BF16),
             pltpu.VMEM((7, BLK, DIM), BF16),
             pltpu.VMEM((BLK, DIM), F32),

time: 35.4 us -> 37 us (1.045); the launches traced: 35.3 us -> 36.5 us
  Pallas kernels: 34.7 us -> 35.8 us
    pallas_call x1, Pallas kernels: 33.9 us -> 35.1 us  [shards(): pl.pallas_call(kernel, out_shape=(pltpu.VMEM((BLK, DIM), F32), pltpu.VMEM...]
where the time goes in v8:
time: 37 us; the launch traced here: 36.5 us
  Pallas kernels  35.8 us (97%)
  between operations  0.64 us (2%)
    pallas_call x1, Pallas kernels, shards(): pl.pallas_call(kernel, out_shape=(pltpu.VMEM((BLK, DIM), F32), pltpu.VMEM...  35.1 us

profile of v8, /device:TPU:1, one launch (start us, length us, event | category | flops | bytes accessed | tf_op | source)
XLA Modules:
  0.0 36.5 jit_solution(5950690582321944851)
XLA Ops:
  0.6 35.1 %shard_map.50 = (f32[256,128]{1,0:T(8,128)S(1)}, f32[1,256,128]{2,1,0:T(8,128)S(1)}) custom-call(bf16[4096,128]{1,0:T(8,128)(2,1)} %q_ref.1, bf16[2048,128]{1,0:T(8,128)(2,1)} %d_ref.1, f32[128]{0:T(128)} %cot_ref.1), custom_call_target="tpu_custom_call" | custom-call | tf_op jit(solution)/shard_map/pallas_call | solution.py:325
  35.8 0.7 %shard_map.51 = (f32[256,128]{1,0:T(8,128)}, f32[1,256,128]{2,1,0:T(8,128)}) custom-call(f32[256,128]{1,0:T(8,128)S(1)} %get-tuple-element.4.gq_in, f32[1,256,128]{2,1,0:T(8,128)S(1)} %get-tuple-element.5.gd_in), custom_call_target="tpu_custom_call" | custom-call | tf_op jit(solution)/shard_map/pallas_call | solution.py:359

commit v9 on v5

--- a/solution.py
+++ b/solution.py
@@ -256,13 +256,14 @@
         send(st)
     lax.fori_loop(1, 3, step_c(1 - zh0), 0)
     d_own[...] = docs_of(3, 1 - zh0)
-    lax.fori_loop(4, 7, step_c(zh0), 0)
+    lax.fori_loop(4, 6, step_c(zh0), 0)
     total = d_own[...]
     for m in range(3):
         d_copy(m).wait_recv()
         total = total + d_in[m].astype(F32)
     d_out[3] = total.astype(BF16)
     d_copy(Z_COPY).start()
+    lax.fori_loop(6, 7, step_c(zh0), 0)
     d_own[...] = docs_of(7, zh0)
 
     mine = jnp.where(lax.rem(y0 + z0, 2) == 0, 3, 7)

time: 35.4 us -> 35.4 us (level)
  no operation moved by 1% of the time
where the time goes in v9:
time: 35.4 us; the launch traced here: 35.3 us
  Pallas kernels  34.7 us (98%)
  between operations  0.64 us (2%)
    pallas_call x1, Pallas kernels, shards(): pl.pallas_call(kernel, out_shape=(pltpu.VMEM((BLK, DIM), F32), pltpu.VMEM...  33.9 us
    pallas_call x1, Pallas kernels, shards(): pl.pallas_call(put_out, out_shape=(jax.ShapeDtypeStruct((BLK, DIM), F32),...  0.72 us

profile of v9, /device:TPU:1, one launch (start us, length us, event | category | flops | bytes accessed | tf_op | source)
XLA Modules:
  0.0 35.3 jit_solution(978067697006533469)
XLA Ops:
  0.6 33.9 %shard_map.50 = (f32[256,128]{1,0:T(8,128)S(1)}, f32[1,256,128]{2,1,0:T(8,128)S(1)}) custom-call(bf16[4096,128]{1,0:T(8,128)(2,1)} %q_ref.1, bf16[2048,128]{1,0:T(8,128)(2,1)} %d_ref.1, f32[128]{0:T(128)} %cot_ref.1), custom_call_target="tpu_custom_call" | custom-call | tf_op jit(solution)/shard_map/pallas_call | solution.py:320
  34.6 0.7 %shard_map.51 = (f32[256,128]{1,0:T(8,128)}, f32[1,256,128]{2,1,0:T(8,128)}) custom-call(f32[256,128]{1,0:T(8,128)S(1)} %get-tuple-element.4.gq_in, f32[1,256,128]{2,1,0:T(8,128)S(1)} %get-tuple-element.5.gd_in), custom_call_target="tpu_custom_call" | custom-call | tf_op jit(solution)/shard_map/pallas_call | solution.py:353
